TPU v7x, 256 devices: a whole 4x4x8 slice. The times are simulated.
256 devices in a mesh: seq: 16 (over y_hi, x, core), rep: 16 (over y_lo, z).
Axes of the slice: x: 4, y: 4 (y_hi: 2, y_lo: 2; y = y_hi * 2 + y_lo), z: 8, core: 2. Of those that a mesh axis runs over, the one named last changes fastest.
Arguments:
- query_rows: bfloat16 [32, 16, 256, 1152], P('rep', 'seq'), as said below
- key_rows: bfloat16 [32, 16, 256, 1152], P('rep', 'seq'), as said below
- value_rows: bfloat16 [32, 16, 256, 1152], P('rep', 'seq'), may hold values from -6 to 6
- out_grad: bfloat16 [32, 16, 256, 1152], P('rep', 'seq'), may hold values from -6 to 6
- out_weight: bfloat16 [1152, 1152], replicated, may hold values from -0.1875 to 0.1875
- frame_count: int32 [32], P('rep'), may hold values from 1 to 16, as said below
- pos_count: int32 [32], P('rep'), may hold values from 64 to 256, as said below
Outputs:
- projected: bfloat16 [32, 16, 256, 1152], P('rep', 'seq')
- grad_query: bfloat16 [32, 16, 256, 1152], P('rep', 'seq')
- grad_key: bfloat16 [32, 16, 256, 1152], P('rep', 'seq')
- grad_value: bfloat16 [32, 16, 256, 1152], P('rep', 'seq')
- grad_weight: float32 [1152, 1152], P('seq')
Inputs may be any that keep to these rules, and one draw needn't show every extreme that they name: `query_rows`: entries lie within -40 to 40. `key_rows`: entries lie within -40 to 40. `frame_count`: some clip has all 16 frames live. `pos_count`: some clip has all 256 positions live.
All inputs are finite; a program needn't handle non-finite values.
Results may differ from a plain program's by a relative error of at most 0.0057.
Values may be sent and summed in bfloat16 or wider, within the bound.
A program may use at most 128 MiB of HBM per device.

v0:
```python
import math

import jax
import jax.numpy as jnp
from jax import lax
from jax.sharding import PartitionSpec as P

HEADS = 16


def attend_local(query_part, key_part, value_part, key_live, row_live):
    nframe, npos_part, width = query_part.shape
    head_dim = width // HEADS
    inv_root = 1.0 / math.sqrt(head_dim)
    shape_heads = (nframe, npos_part, HEADS, head_dim)
    query_heads = query_part.reshape(shape_heads)
    key_heads = key_part.reshape(shape_heads)
    value_heads = value_part.reshape(shape_heads)
    scores = (
        jnp.einsum("fphd,tphd->phft", query_heads, key_heads, preferred_element_type=jnp.float32)
        * inv_root
    )
    scores = jnp.where(key_live, scores, -1e30)
    highest = jnp.max(scores, axis=-1, keepdims=True)
    expo = jnp.exp(scores - highest) * key_live.astype(jnp.float32)
    weights = expo / jnp.sum(expo, axis=-1, keepdims=True)
    rounded = weights.astype(jnp.bfloat16)
    mixed = jnp.einsum("phft,tphd->fphd", rounded, value_heads, preferred_element_type=jnp.float32)
    attn_out = jnp.where(row_live[:, :, None], mixed.reshape(nframe, npos_part, width), 0.0).astype(
        jnp.bfloat16
    )
    return (attn_out, weights, rounded)


def attend_back(query_part, key_part, value_part, cot_part, weights, rounded):
    nframe, npos_part, width = query_part.shape
    head_dim = width // HEADS
    inv_root = 1.0 / math.sqrt(head_dim)
    shape_heads = (nframe, npos_part, HEADS, head_dim)
    cot_heads = cot_part.reshape(shape_heads)
    value_heads = value_part.reshape(shape_heads)
    grad_value = jnp.einsum(
        "phft,fphd->tphd", rounded, cot_heads, preferred_element_type=jnp.float32
    )
    grad_attn = jnp.einsum(
        "fphd,tphd->phft", cot_heads, value_heads, preferred_element_type=jnp.float32
    )
    row_delta = jnp.sum(weights * grad_attn, axis=-1, keepdims=True)
    grad_score = weights * (grad_attn - row_delta) * inv_root
    key_wide = key_part.astype(jnp.float32).reshape(shape_heads)
    query_wide = query_part.astype(jnp.float32).reshape(shape_heads)
    grad_query = jnp.einsum(
        "phft,tphd->fphd", grad_score, key_wide, precision=lax.Precision.HIGHEST
    )
    grad_key = jnp.einsum(
        "phft,fphd->tphd", grad_score, query_wide, precision=lax.Precision.HIGHEST
    )
    full = (nframe, npos_part, width)
    return (
        grad_query.reshape(full).astype(jnp.bfloat16),
        grad_key.reshape(full).astype(jnp.bfloat16),
        grad_value.reshape(full).astype(jnp.bfloat16),
    )


def reduce_weight(flat_grad, flat_out):
    width = flat_grad.shape[1]
    row_share = width // lax.axis_size("seq")
    partial_term = lax.dot_general(
        flat_grad, flat_out, (((0,), (0,)), ((), ())), preferred_element_type=jnp.float32
    )
    total = lax.psum(partial_term, ("seq", "rep"))
    return lax.dynamic_slice_in_dim(total, lax.axis_index("seq") * row_share, row_share, 0)


def shards(query_rows, key_rows, value_rows, out_grad, out_weight, frame_count, pos_count):
    clip_local, frame_local, npos_all, width = query_rows.shape
    rank = lax.axis_index("seq")
    query_pos, key_pos, value_pos = (
        lax.all_to_all(query_rows, "seq", split_axis=2, concat_axis=1, tiled=True),
        lax.all_to_all(key_rows, "seq", split_axis=2, concat_axis=1, tiled=True),
        lax.all_to_all(value_rows, "seq", split_axis=2, concat_axis=1, tiled=True),
    )
    nframe = query_pos.shape[1]
    npos_part = query_pos.shape[2]
    frame_ids = jnp.arange(nframe, dtype=jnp.int32)
    position_ids = rank * npos_part + jnp.arange(npos_part, dtype=jnp.int32)
    key_live = frame_ids[None, :] < frame_count[:, None]
    row_live = key_live[:, :, None] & (position_ids[None, None, :] < pos_count[:, None, None])
    attn_pos, weights, rounded = jax.vmap(attend_local)(
        query_pos, key_pos, value_pos, key_live, row_live
    )
    attn_frames = lax.all_to_all(attn_pos, "seq", split_axis=1, concat_axis=2, tiled=True)
    flat_out = attn_frames.reshape(-1, width)
    flat_grad = out_grad.reshape(-1, width)
    projected = lax.dot_general(
        flat_out, out_weight, (((1,), (1,)), ((), ())), preferred_element_type=jnp.float32
    )
    projected = projected.astype(jnp.bfloat16).reshape(query_rows.shape)
    own_frames = rank * frame_local + jnp.arange(frame_local, dtype=jnp.int32)
    frame_alive = own_frames[None, :, None] < frame_count[:, None, None]
    place_alive = jnp.arange(npos_all, dtype=jnp.int32)[None, None, :] < pos_count[:, None, None]
    out_cot = jnp.dot(flat_grad, out_weight, preferred_element_type=jnp.float32).reshape(
        query_rows.shape
    )
    out_cot = jnp.where((frame_alive & place_alive)[..., None], out_cot, 0.0).astype(jnp.bfloat16)
    cot_pos = lax.all_to_all(out_cot, "seq", split_axis=2, concat_axis=1, tiled=True)
    grad_query_pos, grad_key_pos, grad_value_pos = jax.vmap(attend_back)(
        query_pos, key_pos, value_pos, cot_pos, weights, rounded
    )
    grad_query, grad_key, grad_value = (
        lax.all_to_all(grad_query_pos, "seq", split_axis=1, concat_axis=2, tiled=True),
        lax.all_to_all(grad_key_pos, "seq", split_axis=1, concat_axis=2, tiled=True),
        lax.all_to_all(grad_value_pos, "seq", split_axis=1, concat_axis=2, tiled=True),
    )
    grad_weight = reduce_weight(flat_grad, flat_out)
    return (projected, grad_query, grad_key, grad_value, grad_weight)


def solution(mesh):
    in_specs = (
        P("rep", "seq", None, None),
        P("rep", "seq", None, None),
        P("rep", "seq", None, None),
        P("rep", "seq", None, None),
        P(),
        P("rep"),
        P("rep"),
    )
    out_specs = (
        P("rep", "seq", None, None),
        P("rep", "seq", None, None),
        P("rep", "seq", None, None),
        P("rep", "seq", None, None),
        P("seq", None),
    )
    return jax.shard_map(shards, mesh=mesh, in_specs=in_specs, out_specs=out_specs, check_vma=False)
```

profile of v0, /device:TPU:24, one launch (start us, length us, event | category | flops | bytes accessed | tf_op | source)
XLA Modules:
  0.0 458.3 jit_solution(16041298937253070344)
XLA Ops:
  10.8 7.4 %all-to-all-start = ((bf16[2,1,256,1152]{3,0,1,2:T(2,128)(2,1)}), bf16[2,1,256,1152]{3,0,1,2:T(2,128)(2,1)}, u32[]{:S(2)}, u32[]{:S(2)}) async-start(bf16[2,1,256,1152]{3,0,1,2:T(2,128)(2,1)} %copy.97), calls=%async_computation | async-start | bytes 2359296 | tf_op jit(solution)/shard_map/all_to_all | solution.py:80
  21.8 13.1 %all-to-all-done = bf16[2,1,256,1152]{3,0,1,2:T(2,128)(2,1)} async-done(((bf16[2,1,256,1152]{3,0,1,2:T(2,128)(2,1)}), bf16[2,1,256,1152]{3,0,1,2:T(2,128)(2,1)}, u32[]{:S(2)}, u32[]{:S(2)}) %all-to-all-start) | async-done | bytes 1179680 | tf_op jit(solution)/shard_map/all_to_all | solution.py:80
  34.9 7.1 %all-to-all-start.1 = ((bf16[2,1,256,1152]{3,0,1,2:T(2,128)(2,1)}), bf16[2,1,256,1152]{3,0,1,2:T(2,128)(2,1)}, u32[]{:S(2)}, u32[]{:S(2)}) async-start(bf16[2,1,256,1152]{3,0,1,2:T(2,128)(2,1)} %copy.99), calls=%async_computation.1 | async-start | bytes 2359296 | tf_op jit(solution)/shard_map/all_to_all | solution.py:81
  49.8 8.8 %all-to-all-done.1 = bf16[2,1,256,1152]{3,0,1,2:T(2,128)(2,1)} async-done(((bf16[2,1,256,1152]{3,0,1,2:T(2,128)(2,1)}), bf16[2,1,256,1152]{3,0,1,2:T(2,128)(2,1)}, u32[]{:S(2)}, u32[]{:S(2)}) %all-to-all-start.1) | async-done | bytes 1179680 | tf_op jit(solution)/shard_map/all_to_all | solution.py:81
  58.6 7.5 %all-to-all-start.2 = ((bf16[2,1,256,1152]{3,0,1,2:T(2,128)(2,1)}), bf16[2,1,256,1152]{3,0,1,2:T(2,128)(2,1)}, u32[]{:S(2)}, u32[]{:S(2)}) async-start(bf16[2,1,256,1152]{3,0,1,2:T(2,128)(2,1)} %copy.103), calls=%async_computation.2 | async-start | bytes 2359296 | tf_op jit(solution)/shard_map/all_to_all | solution.py:82
  66.2 6.5 %reshape.212 = bf16[2,16,16,16,72]{4,3,0,2,1:T(8,128)(2,1)} reshape(bf16[2,1,256,1152]{3,0,1,2:T(2,128)(2,1)} %all-to-all-done) | data formatting | bytes 2359296 | tf_op jit(solution)/shard_map/vmap()/reshape | solution.py:16
  72.7 6.5 %reshape.213 = bf16[2,16,16,16,72]{4,3,0,2,1:T(8,128)(2,1)} reshape(bf16[2,1,256,1152]{3,0,1,2:T(2,128)(2,1)} %all-to-all-done.1) | data formatting | bytes 2359296 | tf_op jit(solution)/shard_map/vmap()/reshape | solution.py:17
  79.2 4.7 %fusion.14 = f32[2,16,16,16,16]{3,4,2,1,0:T(8,128)S(1)} fusion(bf16[2,16,16,16,72]{4,3,0,2,1:T(8,128)(2,1)} %reshape.213, bf16[2,16,16,16,72]{4,3,0,2,1:T(8,128)(2,1)} %reshape.212), kind=kOutput, calls=%fused_computation.27 | convolution fusion | flops 18874368 | bytes 2883584 | tf_op jit(solution)/shard_map/vmap(fphd,tphd->phft)/dot_general | solution.py:20
  87.9 7.6 %all-to-all-start.4 = ((bf16[2,1,256,1152]{3,0,1,2:T(2,128)(2,1)}), bf16[2,1,256,1152]{3,0,1,2:T(2,128)(2,1)}, u32[]{:S(2)}, u32[]{:S(2)}) async-start(bf16[2,1,256,1152]{3,0,1,2:T(2,128)(2,1)} %copy.110), calls=%async_computation.4 | async-start | bytes 2359296 | tf_op jit(solution)/shard_map/all_to_all | solution.py:107
  95.5 6.5 %reshape.214 = bf16[2,16,16,16,72]{4,3,0,2,1:T(8,128)(2,1)} reshape(bf16[2,1,256,1152]{3,0,1,2:T(2,128)(2,1)} %all-to-all-done.2) | data formatting | bytes 2359296 | tf_op jit(solution)/shard_map/vmap()/reshape | solution.py:18
  108.5 4.6 reshape.203
  115.7 7.6 %all-to-all-start.3 = ((bf16[2,16,16,1152]{3,2,0,1:T(8,128)(2,1)}), bf16[2,16,16,1152]{3,2,0,1:T(8,128)(2,1)}, u32[]{:S(2)}, u32[]{:S(2)}) async-start(bf16[2,16,16,1152]{3,2,0,1:T(8,128)(2,1)} %copy.108), calls=%async_computation.3 | async-start | bytes 2359296 | tf_op jit(solution)/shard_map/all_to_all | solution.py:93
  123.3 6.5 %reshape.215 = bf16[2,16,16,16,72]{4,3,0,2,1:T(8,128)(2,1)} reshape(bf16[2,1,256,1152]{3,0,1,2:T(2,128)(2,1)} %all-to-all-done.4) | data formatting | bytes 2359296 | tf_op jit(solution)/shard_map/vmap()/reshape | solution.py:40
  136.1 4.6 reshape.211
  140.7 8.6 %multiply_reduce_fusion = (f32[2,16,16,16]{3,2,1,0:T(8,128)S(1)}, f32[2,16,16,16,16]{3,4,2,1,0:T(8,128)}) fusion(f32[2,16,16,16,16]{3,4,2,1,0:T(8,128)} %get-tuple-element.33, f32[2,16,16,16]{3,2,1,0:T(8,128)S(1)} %get-tuple-element.32, bf16[2,16,16,16,72]{4,3,0,2,1:T(8,128)(2,1)} %reshape.214, bf16[2,16,16,16,72]{4,3,0,2,1:T(8,128)(2,1)} %reshape.215), kind=kOutput, calls=%fused_computation.3 | convolution fusion | flops 19259392 | bytes 3473408 | tf_op jit(solution)/shard_map/vmap(fphd,tphd->phft)/dot_general | solution.py:45
  149.3 7.2 %all-to-all-start.7 = ((bf16[2,16,16,1152]{3,2,0,1:T(8,128)(2,1)}), bf16[2,16,16,1152]{3,2,0,1:T(8,128)(2,1)}, u32[]{:S(2)}, u32[]{:S(2)}) async-start(bf16[2,16,16,1152]{3,2,0,1:T(8,128)(2,1)} %reshape.211), calls=%async_computation.7 | async-start | bytes 2359296 | tf_op jit(solution)/shard_map/all_to_all | solution.py:114
  163.5 7.9 %convert_bitcast_fusion.1 = bf16[2,16,16,16,72]{4,1,3,2,0:T(8,128)(2,1)S(1)} fusion(bf16[2,16,16,16,72]{4,3,0,2,1:T(8,128)(2,1)} %reshape.212, f32[2,16,16,16,16]{3,4,2,1,0:T(8,128)} %get-tuple-element.35, f32[2,16,16,16]{3,2,1,0:T(8,128)S(1)} %get-tuple-element.34, f32[2,16,16,16,16]{3,4,2,1,0:T(8,128)} %get-tuple-element.33, ...), kind=kOutput, calls=%fused_computation.15 | convolution fusion | flops 114360320 | bytes 3473408 | tf_op jit(solution)/shard_map/vmap(phft,fphd->tphd)/dot_general | solution.py:55
  173.4 4.6 reshape.210
  178.0 7.2 %all-to-all-start.6 = ((bf16[2,16,16,1152]{3,2,0,1:T(8,128)(2,1)}), bf16[2,16,16,1152]{3,2,0,1:T(8,128)(2,1)}, u32[]{:S(2)}, u32[]{:S(2)}) async-start(bf16[2,16,16,1152]{3,2,0,1:T(8,128)(2,1)} %reshape.210), calls=%async_computation.6 | async-start | bytes 2359296 | tf_op jit(solution)/shard_map/all_to_all | solution.py:113
  185.2 7.5 %convert_bitcast_fusion.2 = bf16[2,16,16,16,72]{4,1,3,2,0:T(8,128)(2,1)S(1)} fusion(bf16[2,16,16,16,72]{4,3,0,2,1:T(8,128)(2,1)} %reshape.213, f32[2,16,16,16,16]{3,4,2,1,0:T(8,128)} %get-tuple-element.35, f32[2,16,16,16]{3,2,1,0:T(8,128)S(1)} %get-tuple-element.34, f32[2,16,16,16,16]{3,4,2,1,0:T(8,128)} %get-tuple-element.33, ...), kind=kOutput, calls=%fused_computation.16 | convolution fusion | flops 114360320 | bytes 3473408 | tf_op jit(solution)/shard_map/vmap(phft,tphd->fphd)/dot_general | solution.py:52
  194.6 4.6 %reshape.209 = bf16[2,16,16,1152]{3,2,0,1:T(8,128)(2,1)} reshape(bf16[2,16,16,16,72]{4,3,2,0,1:T(8,128)(2,1)} %copy.134) | data formatting | bytes 2359296 | tf_op jit(solution)/shard_map/vmap()/convert_element_type | solution.py:60
  203.4 7.5 %all-to-all-start.5 = ((bf16[2,16,16,1152]{3,2,0,1:T(8,128)(2,1)}), bf16[2,16,16,1152]{3,2,0,1:T(8,128)(2,1)}, u32[]{:S(2)}, u32[]{:S(2)}) async-start(bf16[2,16,16,1152]{3,2,0,1:T(8,128)(2,1)} %reshape.209), calls=%async_computation.5 | async-start | bytes 2359296 | tf_op jit(solution)/shard_map/all_to_all | solution.py:112
  215.6 13.0 %all-to-all-done.5 = bf16[2,16,16,1152]{3,2,0,1:T(8,128)(2,1)} async-done(((bf16[2,16,16,1152]{3,2,0,1:T(8,128)(2,1)}), bf16[2,16,16,1152]{3,2,0,1:T(8,128)(2,1)}, u32[]{:S(2)}, u32[]{:S(2)}) %all-to-all-start.5) | async-done | bytes 1179680 | tf_op jit(solution)/shard_map/all_to_all | solution.py:112
  234.0 214.5 %all-reduce.2.cloned.1.call-done = f32[1152,1152]{0,1:T(8,128)} async-done(((f32[1152,1152]{0,1:T(8,128)}), f32[1152,1152]{0,1:T(8,128)}) %all-reduce.2.cloned.1.call-update) | async-done | bytes 5308432 | tf_op jit(solution)/shard_map/psum | solution.py:72
  (49 shorter events, 61.9 us)
Async XLA Ops:
  7.2 34.9 %copy-start = (bf16[1152,1152]{1,0:T(8,128)(2,1)S(1)}, bf16[1152,1152]{1,0:T(8,128)(2,1)}, u32[]{:S(2)}) copy-start(bf16[1152,1152]{1,0:T(8,128)(2,1)} %param.11) | copy-start | bytes 7962628
  10.8 10.9 %copy-start.6 = (s32[2]{0:T(128)S(1)}, s32[2]{0:T(128)}, u32[]{:S(2)}) copy-start(s32[2]{0:T(128)} %param.12) | copy-start | bytes 28
  10.8 24.0 %all-to-all-start = ((bf16[2,1,256,1152]{3,0,1,2:T(2,128)(2,1)}), bf16[2,1,256,1152]{3,0,1,2:T(2,128)(2,1)}, u32[]{:S(2)}, u32[]{:S(2)}) async-start(bf16[2,1,256,1152]{3,0,1,2:T(2,128)(2,1)} %copy.97), calls=%async_computation | async-start | bytes 2359296 | tf_op jit(solution)/shard_map/all_to_all | solution.py:80
  18.2 23.8 %copy-start.5 = (s32[2]{0:T(128)S(1)}, s32[2]{0:T(128)}, u32[]{:S(2)}) copy-start(s32[2]{0:T(128)} %param.13) | copy-start | bytes 28
  34.9 23.7 %all-to-all-start.1 = ((bf16[2,1,256,1152]{3,0,1,2:T(2,128)(2,1)}), bf16[2,1,256,1152]{3,0,1,2:T(2,128)(2,1)}, u32[]{:S(2)}, u32[]{:S(2)}) async-start(bf16[2,1,256,1152]{3,0,1,2:T(2,128)(2,1)} %copy.99), calls=%async_computation.1 | async-start | bytes 2359296 | tf_op jit(solution)/shard_map/all_to_all | solution.py:81
  45.2 2.2 copy-start.3
  58.6 29.3 %all-to-all-start.2 = ((bf16[2,1,256,1152]{3,0,1,2:T(2,128)(2,1)}), bf16[2,1,256,1152]{3,0,1,2:T(2,128)(2,1)}, u32[]{:S(2)}, u32[]{:S(2)}) async-start(bf16[2,1,256,1152]{3,0,1,2:T(2,128)(2,1)} %copy.103), calls=%async_computation.2 | async-start | bytes 2359296 | tf_op jit(solution)/shard_map/all_to_all | solution.py:82
  87.9 27.8 %all-to-all-start.4 = ((bf16[2,1,256,1152]{3,0,1,2:T(2,128)(2,1)}), bf16[2,1,256,1152]{3,0,1,2:T(2,128)(2,1)}, u32[]{:S(2)}, u32[]{:S(2)}) async-start(bf16[2,1,256,1152]{3,0,1,2:T(2,128)(2,1)} %copy.110), calls=%async_computation.4 | async-start | bytes 2359296 | tf_op jit(solution)/shard_map/all_to_all | solution.py:107
  115.7 33.6 %all-to-all-start.3 = ((bf16[2,16,16,1152]{3,2,0,1:T(8,128)(2,1)}), bf16[2,16,16,1152]{3,2,0,1:T(8,128)(2,1)}, u32[]{:S(2)}, u32[]{:S(2)}) async-start(bf16[2,16,16,1152]{3,2,0,1:T(8,128)(2,1)} %copy.108), calls=%async_computation.3 | async-start | bytes 2359296 | tf_op jit(solution)/shard_map/all_to_all | solution.py:93
  149.3 28.7 %all-to-all-start.7 = ((bf16[2,16,16,1152]{3,2,0,1:T(8,128)(2,1)}), bf16[2,16,16,1152]{3,2,0,1:T(8,128)(2,1)}, u32[]{:S(2)}, u32[]{:S(2)}) async-start(bf16[2,16,16,1152]{3,2,0,1:T(8,128)(2,1)} %reshape.211), calls=%async_computation.7 | async-start | bytes 2359296 | tf_op jit(solution)/shard_map/all_to_all | solution.py:114
  156.6 291.9 %all-reduce.2.cloned.1.call-start = ((), (), s32[]{:S(2)}) async-start(), calls=%async_computation.8 | async-start | bytes 10616832 | tf_op jit(solution)/shard_map/psum | solution.py:72
  156.9 2.5 copy-start.4
  158.4 1.0 copy-start.1
  178.0 25.4 %all-to-all-start.6 = ((bf16[2,16,16,1152]{3,2,0,1:T(8,128)(2,1)}), bf16[2,16,16,1152]{3,2,0,1:T(8,128)(2,1)}, u32[]{:S(2)}, u32[]{:S(2)}) async-start(bf16[2,16,16,1152]{3,2,0,1:T(8,128)(2,1)} %reshape.210), calls=%async_computation.6 | async-start | bytes 2359296 | tf_op jit(solution)/shard_map/all_to_all | solution.py:113
  203.4 25.2 %all-to-all-start.5 = ((bf16[2,16,16,1152]{3,2,0,1:T(8,128)(2,1)}), bf16[2,16,16,1152]{3,2,0,1:T(8,128)(2,1)}, u32[]{:S(2)}, u32[]{:S(2)}) async-start(bf16[2,16,16,1152]{3,2,0,1:T(8,128)(2,1)} %reshape.209), calls=%async_computation.5 | async-start | bytes 2359296 | tf_op jit(solution)/shard_map/all_to_all | solution.py:112
  228.6 2.5 copy-start.2
Sparse Core Ops, SparseCore 0:
  163.7 284.7 all-reduce.1
where the time goes:
time: 466 us; the launch traced here: 458 us
  waiting for transfers between devices  254 us (55%)
  local copies, waits for them, and re-layouts  76.8 us (16%)
  starting transfers between devices  59.5 us (13%)
  matrix products  47.8 us (10%)
  between operations  14.7 us (3%)
  other arithmetic  5.81 us (1%)
    psum x1, waiting for transfers between devices, reduce_weight(): total = lax.psum(partial_term, ('seq', 'rep'))  215 us
    all_to_all x1, waiting for transfers between devices, shards(): lax.all_to_all(query_rows, 'seq', split_axis=2, concat_axis=1, tiled=True)  13.1 us
    all_to_all x1, waiting for transfers between devices, shards(): lax.all_to_all(grad_query_pos, 'seq', split_axis=1, concat_axis=2, tiled=...  13 us
    unnamed x18, local copies, waits for them, and re-layouts  11.4 us
  transfers between devices with their start and end apart: 9, of which 5 were waited for; matrix products, arithmetic and copies ran while one was open for 27% of the time, Pallas kernels for 0%

commit v1 on v0

v1 whole, which is shorter than its diff:
```python
import functools
import math

import jax
import jax.numpy as jnp
from jax import lax
from jax.experimental import pallas as pl
from jax.experimental.pallas import tpu as pltpu
from jax.sharding import PartitionSpec as P

HEADS = 16
MESH = pl.DeviceIdType.MESH
VMEM_BYTES = 56 << 20


def greet(n):
    me = lax.axis_index("seq")
    barrier = pltpu.get_barrier_semaphore()

    def signal(j, carry):
        pl.semaphore_signal(
            barrier, inc=1, device_id={"seq": lax.rem(me + j, n)}, device_id_type=MESH
        )
        return carry

    lax.fori_loop(1, n, signal, 0)
    pl.semaphore_wait(barrier, n - 1)
    return me


def to_positions_kernel(n, *refs):
    sources, targets = refs[:4], refs[4:8]
    send, recv, local = refs[8:]
    me = greet(n)
    clips, part = targets[0].shape[0], targets[0].shape[2]
    own = []
    for c in range(clips):
        for a in range(4):
            mine = pl.ds(pl.multiple_of(me * part, part), part)
            copy = pltpu.make_async_copy(
                sources[a].at[c, 0, mine], targets[a].at[c, me], local.at[c, a]
            )
            copy.start()
            own.append(copy)

            def push(j, carry):
                peer = lax.rem(me + j, n)
                theirs = pl.ds(pl.multiple_of(peer * part, part), part)
                pltpu.make_async_remote_copy(
                    src_ref=sources[a].at[c, 0, theirs],
                    dst_ref=targets[a].at[c, me],
                    send_sem=send.at[c, a],
                    recv_sem=recv.at[c, a],
                    device_id={"seq": peer},
                    device_id_type=MESH,
                ).start()
                return carry

            lax.fori_loop(1, n, push, 0)
    for copy in own:
        copy.wait()
    for c in range(clips):
        for a in range(4):
            whole = targets[a].at[c, pl.ds(0, n - 1)]
            pltpu.make_async_copy(whole, whole, recv.at[c, a]).wait()
            pltpu.make_async_copy(whole, whole, send.at[c, a]).wait()


def to_frames_kernel(n, *refs):
    sources, targets = refs[:4], refs[4:8]
    send, recv, local = refs[8:]
    me = greet(n)
    clips, part = sources[0].shape[0], sources[0].shape[2]
    mine = pl.ds(pl.multiple_of(me * part, part), part)
    own = []
    for c in range(clips):
        for a in range(4):
            copy = pltpu.make_async_copy(
                sources[a].at[c, me], targets[a].at[c, 0, mine], local.at[c, a]
            )
            copy.start()
            own.append(copy)

            def push(j, carry):
                peer = lax.rem(me + j, n)
                pltpu.make_async_remote_copy(
                    src_ref=sources[a].at[c, peer],
                    dst_ref=targets[a].at[c, 0, mine],
                    send_sem=send.at[c, a],
                    recv_sem=recv.at[c, a],
                    device_id={"seq": peer},
                    device_id_type=MESH,
                ).start()
                return carry

            lax.fori_loop(1, n, push, 0)
    for copy in own:
        copy.wait()
    for c in range(clips):
        for a in range(4):
            whole = sources[a].at[c, pl.ds(0, n - 1)]
            pltpu.make_async_copy(whole, whole, recv.at[c, a]).wait()
            pltpu.make_async_copy(whole, whole, send.at[c, a]).wait()


def exchange(kernel, n, arrays, out_shape, collective_id):
    clips = arrays[0].shape[0]
    return pl.pallas_call(
        functools.partial(kernel, n),
        out_shape=[jax.ShapeDtypeStruct(out_shape, jnp.bfloat16)] * 4,
        in_specs=[pl.BlockSpec(memory_space=pl.ANY)] * 4,
        out_specs=[pl.BlockSpec(memory_space=pl.ANY)] * 4,
        scratch_shapes=[pltpu.SemaphoreType.DMA((clips, 4))] * 3,
        compiler_params=pltpu.CompilerParams(collective_id=collective_id, has_side_effects=True),
    )(*arrays)


def columns_of(width):
    step = 384 if width % 384 == 0 else width
    return [pl.ds(i, step) for i in range(0, width, step)]


def attend(part, place, frames, places, query, key, value, grad, weight, cot, attn, bias, outs):
    projected, grad_query, grad_key, grad_value = outs
    rows, width = query.shape
    head_dim = width // HEADS
    inv_root = 1.0 / math.sqrt(head_dim)
    row = lax.broadcasted_iota(jnp.int32, (rows, 1), 0)
    live = (row // part < frames) & (place + row % part < places)
    for cols in columns_of(width):
        wide = jnp.dot(grad[...], weight[:, cols], preferred_element_type=jnp.float32)
        cot[:, cols] = jnp.where(live, wide, 0.0).astype(jnp.bfloat16)
    key_row = lax.broadcasted_iota(jnp.int32, (rows, rows), 0)
    query_row = lax.broadcasted_iota(jnp.int32, (rows, rows), 1)
    allowed = (key_row % part == query_row % part) & (key_row // part < frames)
    bias[...] = jnp.where(allowed, 0.0, -1e30)

    def head(h, carry):
        low = jnp.minimum((h * head_dim) // 128 * 128, width - 256)
        window = pl.ds(pl.multiple_of(low, 128), 256)
        lane = lax.broadcasted_iota(jnp.int32, (rows, 256), 1) + low
        inside = (lane >= h * head_dim) & (lane < (h + 1) * head_dim)
        zero = jnp.zeros((rows, 256), jnp.bfloat16)
        key_h, value_h = key[:, window], value[:, window]
        query_h = jnp.where(inside, query[:, window], zero)
        cot_h = jnp.where(inside, cot[:, window], zero)
        scores = lax.dot_general(
            key_h, query_h, (((1,), (1,)), ((), ())), preferred_element_type=jnp.float32
        )
        scores = scores + bias[...]
        highest = jnp.max(scores, axis=0, keepdims=True)
        expo = jnp.exp2((scores - highest) * (inv_root * math.log2(math.e)))
        weights = expo * (1.0 / jnp.sum(expo, axis=0, keepdims=True))
        rounded = weights.astype(jnp.bfloat16)
        mixed = lax.dot_general(
            rounded, value_h, (((0,), (0,)), ((), ())), preferred_element_type=jnp.float32
        )
        mixed = jnp.where(live, mixed, 0.0).astype(jnp.bfloat16)
        attn[:, window] = jnp.where(inside, mixed, attn[:, window])
        gv = jnp.dot(rounded, cot_h, preferred_element_type=jnp.float32).astype(jnp.bfloat16)
        grad_value[:, window] = jnp.where(inside, gv, grad_value[:, window])
        grad_attn = lax.dot_general(
            value_h, cot_h, (((1,), (1,)), ((), ())), preferred_element_type=jnp.float32
        )
        delta = jnp.sum(weights * grad_attn, axis=0, keepdims=True)
        grad_score = (weights * (grad_attn - delta) * inv_root).astype(jnp.bfloat16)
        gq = lax.dot_general(
            grad_score, key_h, (((0,), (0,)), ((), ())), preferred_element_type=jnp.float32
        ).astype(jnp.bfloat16)
        grad_query[:, window] = jnp.where(inside, gq, grad_query[:, window])
        gk = jnp.dot(grad_score, query_h, preferred_element_type=jnp.float32).astype(jnp.bfloat16)
        grad_key[:, window] = jnp.where(inside, gk, grad_key[:, window])
        return carry

    lax.fori_loop(0, HEADS, head, 0)
    for cols in columns_of(width):
        projected[:, cols] = lax.dot_general(
            attn[...], weight[cols, :], (((1,), (1,)), ((), ())), preferred_element_type=jnp.float32
        ).astype(jnp.bfloat16)


def compute_kernel(part, frames, places, query, key, value, grad, weight, *refs):
    outs, total, (cot, attn, bias) = refs[:4], refs[4], refs[5:]
    c = pl.program_id(0)
    place = lax.axis_index("seq") * part
    squeeze = [r.at[0] for r in (query, key, value, grad)]
    attend(
        part, place, frames[c], places[c], *squeeze, weight, cot, attn, bias,
        [r.at[0] for r in outs],
    )

    @pl.when(c == 0)
    def _():
        total[...] = jnp.zeros_like(total)

    for rows in columns_of(total.shape[0]):
        total[rows, :] += lax.dot_general(
            grad[0, :, rows], attn[...], (((0,), (0,)), ((), ())),
            preferred_element_type=jnp.float32,
        )


def compute(arrays, weight, frames, places, part):
    clips, rows, width = arrays[0].shape
    block = pl.BlockSpec((1, rows, width), lambda c: (c, 0, 0))
    fixed = pl.BlockSpec((width, width), lambda c: (0, 0))
    smem = pl.BlockSpec(memory_space=pltpu.SMEM)
    shape = jax.ShapeDtypeStruct((clips, rows, width), jnp.bfloat16)
    return pl.pallas_call(
        functools.partial(compute_kernel, part),
        grid=(clips,),
        out_shape=[shape] * 4 + [jax.ShapeDtypeStruct((width, width), jnp.float32)],
        in_specs=[smem, smem] + [block] * 4 + [fixed],
        out_specs=[block] * 4 + [fixed],
        scratch_shapes=[
            pltpu.VMEM((rows, width), jnp.bfloat16),
            pltpu.VMEM((rows, width), jnp.bfloat16),
            pltpu.VMEM((rows, rows), jnp.float32),
        ],
        compiler_params=pltpu.CompilerParams(vmem_limit_bytes=VMEM_BYTES),
    )(frames, places, *arrays, weight)


def shards(query_rows, key_rows, value_rows, out_grad, out_weight, frame_count, pos_count):
    clips, _, places, width = query_rows.shape
    n = lax.axis_size("seq")
    part = places // n
    moved = exchange(
        to_positions_kernel,
        n,
        (query_rows, key_rows, value_rows, out_grad),
        (clips, n, part, width),
        0,
    )
    moved = [m.reshape(clips, n * part, width) for m in moved]
    *results, partial_term = compute(moved, out_weight, frame_count, pos_count, part)
    results = [r.reshape(clips, n, part, width) for r in results]
    grad_weight = lax.psum_scatter(partial_term, "seq", scatter_dimension=0, tiled=True)
    grad_weight = lax.psum(grad_weight, "rep")
    back = exchange(to_frames_kernel, n, results, (clips, 1, places, width), 1)
    return (*back, grad_weight)


def solution(mesh):
    rows = P("rep", "seq", None, None)
    return jax.shard_map(
        shards,
        mesh=mesh,
        in_specs=(rows, rows, rows, rows, P(), P("rep"), P("rep")),
        out_specs=(rows, rows, rows, rows, P("seq", None)),
        check_vma=False,
    )
```

time: 466 us -> 350 us (0.75); the launches traced: 458 us -> 348 us
  Pallas kernels: 0 us -> 154 us
  waiting for transfers between devices: 254 us -> 173 us
  local copies, waits for them, and re-layouts: 76.8 us -> 7.66 us
  starting transfers between devices: 59.5 us -> 0.08 us
  matrix products: 47.8 us -> 0 us
  other arithmetic: 5.81 us -> 0 us
    pallas_call x0 -> x3, Pallas kernels: none -> 154 us  [the longest x2 118 us: exchange(): pl.pallas_call(functools.partial(kernel, n), out_shape=[jax.ShapeDtypeStr...]
    psum x1, waiting for transfers between devices: 215 us -> 78.7 us  [shards(): grad_weight = lax.psum(grad_weight, 'rep')]
    unnamed x1 -> x3, waiting for transfers between devices: 0.02 us -> 94.2 us
    all_to_all x8 -> x0, starting transfers between devices: 59.2 us -> none  [the longest x1 7.62 us: shards(): lax.all_to_all(attn_pos, 'seq', split_axis=1, concat_axis=2, tiled=True)]
    dot_general x9 -> x0, matrix products: 47.8 us -> none  [the longest x1 8.62 us: attend_back(): jnp.einsum('fphd,tphd->phft', cot_heads, value_heads, preferred_element_t...]
    all_to_all x8 -> x0, waiting for transfers between devices: 39.1 us -> none  [the longest x1 13.1 us: shards(): lax.all_to_all(query_rows, 'seq', split_axis=2, concat_axis=1, tiled=True)]
    reshape x5 -> x0, local copies, waits for them, and re-layouts: 30.7 us -> none  [the longest x1 6.53 us: attend_local(): value_heads = value_part.reshape(shape_heads)]
    convert_element_type x8 -> x0, local copies, waits for them, and re-layouts: 22.7 us -> none  [the longest x2 6.48 us: attend_back(): grad_query.reshape(full).astype(jnp.bfloat16)]
  transfers between devices with their start and end apart: 9 -> 2, of which waited for: 5 -> 2; matrix products, arithmetic and copies ran while one was open for 27% -> 0% of each run, Pallas kernels for 0% -> 17%
where the time goes in v1:
time: 350 us; the launch traced here: 348 us
  waiting for transfers between devices  173 us (49%)
  Pallas kernels  154 us (44%)
  between operations  14.1 us (4%)
  local copies, waits for them, and re-layouts  7.66 us (2%)
    pallas_call x2, Pallas kernels, exchange(): pl.pallas_call(functools.partial(kernel, n), out_shape=[jax.ShapeDtypeStr...  118 us
    unnamed x3, waiting for transfers between devices  94.2 us
    psum x1, waiting for transfers between devices, shards(): grad_weight = lax.psum(grad_weight, 'rep')  78.7 us
    pallas_call x1, Pallas kernels, compute(): pl.pallas_call(functools.partial(compute_kernel, part), grid=(clips,), ou...  35.6 us
    unnamed x13, local copies, waits for them, and re-layouts  7.66 us
  transfers between devices with their start and end apart: 2, of which 2 were waited for; matrix products, arithmetic and copies ran while one was open for 0% of the time, Pallas kernels for 17%

profile of v1, /device:TPU:24, one launch (start us, length us, event | category | flops | bytes accessed | tf_op | source)
XLA Modules:
  0.0 348.3 jit_solution(4855362226146395394)
XLA Ops:
  7.2 0.0 reduce-scatter.4.cloned.1.call-start
  7.2 57.9 %shard_map.110 = (bf16[2,16,16,1152]{3,2,1,0:T(8,128)(2,1)}, bf16[2,16,16,1152]{3,2,1,0:T(8,128)(2,1)}, bf16[2,16,16,1152]{3,2,1,0:T(8,128)(2,1)}, bf16[2,16,16,1152]{3,2,1,0:T(8,128)(2,1)}) custom-call(bf16[2,1,256,1152]{3,2,1,0:T(8,128)(2,1)} %refs_0_.1, bf16[2,1,256,1152]{3,2,1,0:T(8,128)(2,1)} %refs_1_.1, bf16[2,1,256,1152]{3,2,1,0:T(8,128)(2,1)} %refs_2_.1, ...), custom_call_target="tpu_custom_call" | custom-call | tf_op jit(solution)/shard_map/pallas_call | solution.py:108
  65.1 35.6 %shard_map.111 = (bf16[2,256,1152]{2,1,0:T(8,128)(2,1)}, bf16[2,256,1152]{2,1,0:T(8,128)(2,1)}, bf16[2,256,1152]{2,1,0:T(8,128)(2,1)}, bf16[2,256,1152]{2,1,0:T(8,128)(2,1)}, f32[1152,1152]{1,0:T(8,128)}) custom-call(s32[2]{0:T(128)} %frames.1, s32[2]{0:T(128)} %places.1, bf16[2,256,1152]{2,1,0:T(8,128)(2,1)} %bitcast.13, bf16[2,256,1152]{2,1,0:T(8,128)(2,1)} %bitcast.14, ...), custom_call_target="tpu_custom_call" | custom-call | tf_op jit(solution)/shard_map/pallas_call | solution.py:209
  100.8 0.0 reduce-scatter.4.cloned.1.call-update
  100.8 0.0 all-reduce.3.cloned.1.call-start
  100.8 94.1 %reduce-scatter.4.cloned.1.call-done = f32[72,1152]{1,0:T(8,128)} async-done(((f32[1152,1152]{1,0:T(8,128)}), f32[72,1152]{1,0:T(8,128)}) %reduce-scatter.4.cloned.1.call-update) | async-done | bytes 331792
  195.0 0.0 all-reduce.3.cloned.1.call-update
  195.0 60.0 %shard_map.112 = (bf16[2,1,256,1152]{3,2,1,0:T(8,128)(2,1)}, bf16[2,1,256,1152]{3,2,1,0:T(8,128)(2,1)}, bf16[2,1,256,1152]{3,2,1,0:T(8,128)(2,1)}, bf16[2,1,256,1152]{3,2,1,0:T(8,128)(2,1)}) custom-call(bf16[2,16,16,1152]{3,2,1,0:T(8,128)(2,1)} %bitcast.9, bf16[2,16,16,1152]{3,2,1,0:T(8,128)(2,1)} %bitcast.10, bf16[2,16,16,1152]{3,2,1,0:T(8,128)(2,1)} %bitcast.11, ...), custom_call_target="tpu_custom_call" | custom-call | tf_op jit(solution)/shard_map/pallas_call | solution.py:108
  255.0 0.0 copy-start.2
  255.1 78.7 %all-reduce.3.cloned.1.call-done = f32[72,1152]{1,0:T(8,128)} async-done(((f32[72,1152]{1,0:T(8,128)}), f32[72,1152]{1,0:T(8,128)}) %all-reduce.3.cloned.1.call-update) | async-done | bytes 331792 | tf_op jit(solution)/shard_map/psum | solution.py:239
  333.8 2.4 copy.17
  336.2 0.0 copy-done.2
  336.2 0.0 copy-start.1
  336.2 1.0 copy.18
  337.2 0.7 copy-done.1
  337.9 0.0 copy-start
  337.9 1.0 copy.19
  338.9 0.7 copy-done
  339.6 0.0 copy-start.3
  339.6 1.0 copy.20
  340.6 0.1 copy-done.3
  340.7 0.7 copy.21
Async XLA Ops:
  7.2 187.8 %reduce-scatter.4.cloned.1.call-start = ((), (), s32[]{:S(2)}) async-start(), calls=%async_computation.2 | async-start | bytes 5640192
  100.8 233.0 %all-reduce.3.cloned.1.call-start = ((), (), s32[]{:S(2)}) async-start(), calls=%async_computation.1 | async-start | bytes 663552 | tf_op jit(solution)/shard_map/psum | solution.py:239
  255.0 81.1 %copy-start.2 = (bf16[2,1,256,1152]{3,2,1,0:T(8,128)(2,1)S(1)}, bf16[2,1,256,1152]{3,2,1,0:T(8,128)(2,1)}, u32[]{:S(2)}) copy-start(bf16[2,1,256,1152]{3,2,1,0:T(8,128)(2,1)} %get-tuple-element.37) | copy-start | bytes 3538948
  336.2 1.7 copy-start.1
  337.9 1.7 copy-start
  339.6 1.2 copy-start.3
Sparse Core Ops, SparseCore 0:
  100.9 94.0 reduce-scatter.3
  197.8 135.9 all-reduce.2

commit v2 on v1

--- a/solution.py
+++ b/solution.py
@@ -9,29 +9,34 @@
 from jax.sharding import PartitionSpec as P
 
 HEADS = 16
+RING = 8
+SLABS = 9
 MESH = pl.DeviceIdType.MESH
 VMEM_BYTES = 56 << 20
 
 
-def greet(n):
-    me = lax.axis_index("seq")
+def greet(peers):
     barrier = pltpu.get_barrier_semaphore()
-
-    def signal(j, carry):
-        pl.semaphore_signal(
-            barrier, inc=1, device_id={"seq": lax.rem(me + j, n)}, device_id_type=MESH
-        )
-        return carry
-
-    lax.fori_loop(1, n, signal, 0)
-    pl.semaphore_wait(barrier, n - 1)
-    return me
+    for first, count, peer_of in peers:
+
+        def signal(j, carry):
+            pl.semaphore_signal(barrier, inc=1, device_id=peer_of(j), device_id_type=MESH)
+            return carry
+
+        lax.fori_loop(first, first + count, signal, 0)
+    pl.semaphore_wait(barrier, sum(count for _, count, _ in peers))
+
+
+def row_peers(n):
+    s, r = lax.axis_index("seq"), lax.axis_index("rep")
+    return (1, n - 1, lambda j: (lax.rem(s + j, n), r))
 
 
 def to_positions_kernel(n, *refs):
     sources, targets = refs[:4], refs[4:8]
     send, recv, local = refs[8:]
-    me = greet(n)
+    me = lax.axis_index("seq")
+    greet([row_peers(n)])
     clips, part = targets[0].shape[0], targets[0].shape[2]
     own = []
     for c in range(clips):
@@ -66,34 +71,206 @@
             pltpu.make_async_copy(whole, whole, send.at[c, a]).wait()
 
 
+def slab_place(slab):
+    block, i = slab // SLABS, slab % SLABS
+    core, chip = block % 2, block // 2
+    return (core, i, chip) if i < RING else (core, chip, RING)
+
+
+class WeightSum:
+    def __init__(self, term, out, half, ring, plane, last, sems):
+        self.term, self.out, self.half, self.ring, self.plane, self.last = (
+            term, out, half, ring, plane, last,
+        )
+        (self.half_sems, self.ring_send, self.ring_recv, self.plane_sems, self.z_sems) = sems
+        self.s, self.r = lax.axis_index("seq"), lax.axis_index("rep")
+        self.core, self.chip = lax.rem(self.s, 2), lax.div(self.s, 2)
+        self.z, self.low = lax.rem(self.r, RING), lax.div(self.r, RING)
+
+    def peers(self):
+        s, r, core, z, low = self.s, self.r, self.core, self.z, self.low
+        return [
+            (0, RING, lambda j: (2 * j + core, (1 - low) * RING + z)),
+            (1, RING - 1, lambda j: (s, low * RING + lax.rem(z + j, RING))),
+        ]
+
+    def half_copy(self):
+        return pltpu.make_async_remote_copy(
+            src_ref=self.term.at[1 - self.core],
+            dst_ref=self.half,
+            send_sem=self.half_sems.at[0],
+            recv_sem=self.half_sems.at[1],
+            device_id=(self.s + 1 - 2 * self.core, self.r),
+            device_id_type=MESH,
+        )
+
+    def add_half(self):
+        self.half_copy().wait()
+
+        def add(j, carry):
+            self.half[j] += self.term[self.core, j]
+            return carry
+
+        lax.fori_loop(0, RING, add, 0)
+
+    def piece(self, t):
+        way = 1 - 2 * self.core
+        return lax.rem(self.z - way * (t + 1) + 2 * RING, RING)
+
+    def ring_copy(self, t):
+        way = 1 - 2 * self.core
+        return pltpu.make_async_remote_copy(
+            src_ref=self.half.at[self.piece(0)] if t == 0 else self.ring.at[t - 1],
+            dst_ref=self.ring.at[t],
+            send_sem=self.ring_send.at[t],
+            recv_sem=self.ring_recv.at[t],
+            device_id=(self.s, self.low * RING + lax.rem(self.z + way + RING, RING)),
+            device_id_type=MESH,
+        )
+
+    def ring_step(self, t):
+        self.ring_copy(t).wait_recv()
+        self.ring[t] += self.half[self.piece(t + 1)]
+        if t + 1 < RING - 1:
+            self.ring_copy(t + 1).start()
+
+    def spread(self, start):
+        held, me = self.ring.at[RING - 2], self.low * RING + self.chip
+
+        def each(j, carry):
+            chip, low = lax.rem(j, RING), lax.div(j, RING)
+            self.plane_copy(held.at[chip], self.plane.at[0, me], 0, 2 * chip + self.core, low, start)
+            return carry
+
+        lax.fori_loop(0, 2 * RING, each, 0)
+        for low in range(2):
+            self.plane_copy(held.at[RING], self.plane.at[1, me], 1, 2 * self.z + self.core, low, start)
+
+    def plane_copy(self, src, dst, k, s, low, start):
+        is_self = (s == self.s) & (low == self.low)
+
+        @pl.when(jnp.logical_not(is_self))
+        def _():
+            copy = pltpu.make_async_remote_copy(
+                src_ref=src,
+                dst_ref=dst,
+                send_sem=self.plane_sems.at[0, k],
+                recv_sem=self.plane_sems.at[1, k],
+                device_id=(s, low * RING + self.z),
+                device_id_type=MESH,
+            )
+            if start:
+                copy.start()
+            else:
+                copy.wait_send()
+
+        if start:
+
+            @pl.when(is_self)
+            def _():
+                self.plane[k, self.low * RING + self.chip] = self.ring[
+                    RING - 2, self.chip if k == 0 else RING
+                ]
+
+    def z_copy(self, k, j):
+        rows = pl.ds(pl.multiple_of(self.z * 8, 8) if k == 0 else RING * 8, 8)
+        return pltpu.make_async_remote_copy(
+            src_ref=self.last.at[k],
+            dst_ref=self.out.at[rows],
+            send_sem=self.z_sems.at[0, k],
+            recv_sem=self.z_sems.at[1, k],
+            device_id=(self.s, self.low * RING + lax.rem(self.z + j, RING)),
+            device_id_type=MESH,
+        )
+
+    def to_all_z(self, k, start):
+        def each(j, carry):
+            copy = self.z_copy(k, j)
+            if start:
+                copy.start()
+            else:
+                copy.wait_send()
+            return carry
+
+        lax.fori_loop(1, RING, each, 0)
+
+    def gather(self):
+        for k in range(2):
+
+            @pl.when((self.chip == self.z) | (k == 0))
+            def _():
+                whole = self.plane.at[k, pl.ds(0, 2 * RING - 1)]
+                pltpu.make_async_copy(whole, whole, self.plane_sems.at[1, k]).wait()
+                total = self.plane[k, 0]
+                for i in range(1, 2 * RING):
+                    total = total + self.plane[k, i]
+                self.last[k] = total
+                self.to_all_z(k, True)
+                rows = pl.ds(pl.multiple_of(self.z * 8, 8) if k == 0 else RING * 8, 8)
+                self.out[rows] = total
+
+    def finish(self):
+        whole = self.plane.at[0, pl.ds(0, RING - 1)]
+        pltpu.make_async_copy(whole, whole, self.z_sems.at[1, 0]).wait()
+        self.to_all_z(0, False)
+
+        @pl.when(self.chip == self.z)
+        def _():
+            self.to_all_z(1, False)
+
+        @pl.when(self.chip != self.z)
+        def _():
+            one = self.plane.at[1, 0]
+            pltpu.make_async_copy(one, one, self.z_sems.at[1, 1]).wait()
+
+        self.spread(False)
+        for t in range(RING - 1):
+            self.ring_copy(t).wait_send()
+
+
 def to_frames_kernel(n, *refs):
-    sources, targets = refs[:4], refs[4:8]
-    send, recv, local = refs[8:]
-    me = greet(n)
+    sources, term, targets, out = refs[:4], refs[4], refs[5:9], refs[9]
+    half, ring, plane, last, send, recv, local = refs[10:17]
+    weight_sum = WeightSum(term, out, half, ring, plane, last, refs[17:])
+    me = lax.axis_index("seq")
+    rep = lax.axis_index("rep")
+    greet([row_peers(n)] + weight_sum.peers())
     clips, part = sources[0].shape[0], sources[0].shape[2]
     mine = pl.ds(pl.multiple_of(me * part, part), part)
     own = []
-    for c in range(clips):
-        for a in range(4):
-            copy = pltpu.make_async_copy(
-                sources[a].at[c, me], targets[a].at[c, 0, mine], local.at[c, a]
-            )
-            copy.start()
-            own.append(copy)
-
-            def push(j, carry):
-                peer = lax.rem(me + j, n)
-                pltpu.make_async_remote_copy(
-                    src_ref=sources[a].at[c, peer],
-                    dst_ref=targets[a].at[c, 0, mine],
-                    send_sem=send.at[c, a],
-                    recv_sem=recv.at[c, a],
-                    device_id={"seq": peer},
-                    device_id_type=MESH,
-                ).start()
-                return carry
-
-            lax.fori_loop(1, n, push, 0)
+
+    def post(c, a):
+        copy = pltpu.make_async_copy(
+            sources[a].at[c, me], targets[a].at[c, 0, mine], local.at[c, a]
+        )
+        copy.start()
+        own.append(copy)
+
+        def push(j, carry):
+            peer = lax.rem(me + j, n)
+            pltpu.make_async_remote_copy(
+                src_ref=sources[a].at[c, peer],
+                dst_ref=targets[a].at[c, 0, mine],
+                send_sem=send.at[c, a],
+                recv_sem=recv.at[c, a],
+                device_id=(peer, rep),
+                device_id_type=MESH,
+            ).start()
+            return carry
+
+        lax.fori_loop(1, n, push, 0)
+
+    weight_sum.half_copy().start()
+    post(0, 0)
+    weight_sum.add_half()
+    weight_sum.ring_copy(0).start()
+    posts = [(c, a) for c in range(clips) for a in range(4)][1:]
+    for t in range(RING - 1):
+        post(*posts[t])
+        weight_sum.ring_step(t)
+    weight_sum.spread(True)
+    weight_sum.gather()
+    weight_sum.finish()
     for copy in own:
         copy.wait()
     for c in range(clips):
@@ -103,16 +280,46 @@
             pltpu.make_async_copy(whole, whole, send.at[c, a]).wait()
 
 
-def exchange(kernel, n, arrays, out_shape, collective_id):
+def to_positions(n, arrays, out_shape):
     clips = arrays[0].shape[0]
     return pl.pallas_call(
-        functools.partial(kernel, n),
+        functools.partial(to_positions_kernel, n),
         out_shape=[jax.ShapeDtypeStruct(out_shape, jnp.bfloat16)] * 4,
         in_specs=[pl.BlockSpec(memory_space=pl.ANY)] * 4,
         out_specs=[pl.BlockSpec(memory_space=pl.ANY)] * 4,
         scratch_shapes=[pltpu.SemaphoreType.DMA((clips, 4))] * 3,
-        compiler_params=pltpu.CompilerParams(collective_id=collective_id, has_side_effects=True),
+        compiler_params=pltpu.CompilerParams(collective_id=0, has_side_effects=True),
     )(*arrays)
+
+
+def to_frames(n, arrays, term, out_shape):
+    clips, width = arrays[0].shape[0], term.shape[-1]
+    dma = pltpu.SemaphoreType.DMA
+    return pl.pallas_call(
+        functools.partial(to_frames_kernel, n),
+        out_shape=[jax.ShapeDtypeStruct(out_shape, jnp.bfloat16)] * 4
+        + [jax.ShapeDtypeStruct((SLABS * 8, width), jnp.float32)],
+        in_specs=[pl.BlockSpec(memory_space=pl.ANY)] * 4 + [pl.BlockSpec(memory_space=pltpu.VMEM)],
+        out_specs=[pl.BlockSpec(memory_space=pl.ANY)] * 4
+        + [pl.BlockSpec(memory_space=pltpu.VMEM)],
+        scratch_shapes=[
+            pltpu.VMEM((RING, SLABS, 8, width), jnp.float32),
+            pltpu.VMEM((RING - 1, SLABS, 8, width), jnp.float32),
+            pltpu.VMEM((2, 2 * RING, 8, width), jnp.float32),
+            pltpu.VMEM((2, 8, width), jnp.float32),
+            dma((clips, 4)),
+            dma((clips, 4)),
+            dma((clips, 4)),
+            dma((2,)),
+            dma((RING - 1,)),
+            dma((RING - 1,)),
+            dma((2, 2)),
+            dma((2, 2)),
+        ],
+        compiler_params=pltpu.CompilerParams(
+            collective_id=1, has_side_effects=True, vmem_limit_bytes=VMEM_BYTES
+        ),
+    )(*arrays, term)
 
 
 def columns_of(width):
@@ -179,66 +386,69 @@
         ).astype(jnp.bfloat16)
 
 
+def weight_term(grad, attn, term):
+    for rows in columns_of(grad.shape[1]):
+        found = lax.dot_general(
+            grad[:, rows], attn[...], (((0,), (0,)), ((), ())), preferred_element_type=jnp.float32
+        )
+        for k in range(rows.size // 8):
+            term[slab_place(rows.start // 8 + k)] = found[8 * k : 8 * k + 8]
+
+
 def compute_kernel(part, frames, places, query, key, value, grad, weight, *refs):
-    outs, total, (cot, attn, bias) = refs[:4], refs[4], refs[5:]
+    outs, term, (cot, attn, bias) = refs[:4], refs[4], refs[5:]
     c = pl.program_id(0)
     place = lax.axis_index("seq") * part
-    squeeze = [r.at[0] for r in (query, key, value, grad)]
+    rows = query.shape[1]
+    mine = pl.ds(pl.multiple_of(c * rows, rows), rows)
     attend(
-        part, place, frames[c], places[c], *squeeze, weight, cot, attn, bias,
-        [r.at[0] for r in outs],
+        part, place, frames[c], places[c],
+        query.at[0], key.at[0], value.at[0], grad.at[mine],
+        weight, cot, attn.at[mine], bias, [r.at[0] for r in outs],
     )
 
-    @pl.when(c == 0)
+    @pl.when(c == pl.num_programs(0) - 1)
     def _():
-        total[...] = jnp.zeros_like(total)
-
-    for rows in columns_of(total.shape[0]):
-        total[rows, :] += lax.dot_general(
-            grad[0, :, rows], attn[...], (((0,), (0,)), ((), ())),
-            preferred_element_type=jnp.float32,
-        )
+        weight_term(grad, attn, term)
 
 
 def compute(arrays, weight, frames, places, part):
     clips, rows, width = arrays[0].shape
     block = pl.BlockSpec((1, rows, width), lambda c: (c, 0, 0))
-    fixed = pl.BlockSpec((width, width), lambda c: (0, 0))
+
+    def fixed(*shape):
+        return pl.BlockSpec(shape, lambda c: (0,) * len(shape))
+
     smem = pl.BlockSpec(memory_space=pltpu.SMEM)
     shape = jax.ShapeDtypeStruct((clips, rows, width), jnp.bfloat16)
+    term_shape = (2, RING, SLABS, 8, width)
+    query, key, value, grad = arrays
     return pl.pallas_call(
         functools.partial(compute_kernel, part),
         grid=(clips,),
-        out_shape=[shape] * 4 + [jax.ShapeDtypeStruct((width, width), jnp.float32)],
-        in_specs=[smem, smem] + [block] * 4 + [fixed],
-        out_specs=[block] * 4 + [fixed],
+        out_shape=[shape] * 4 + [jax.ShapeDtypeStruct(term_shape, jnp.float32)],
+        in_specs=[smem, smem] + [block] * 3 + [fixed(clips * rows, width), fixed(width, width)],
+        out_specs=[block] * 4 + [fixed(*term_shape)],
         scratch_shapes=[
             pltpu.VMEM((rows, width), jnp.bfloat16),
-            pltpu.VMEM((rows, width), jnp.bfloat16),
+            pltpu.VMEM((clips * rows, width), jnp.bfloat16),
             pltpu.VMEM((rows, rows), jnp.float32),
         ],
         compiler_params=pltpu.CompilerParams(vmem_limit_bytes=VMEM_BYTES),
-    )(frames, places, *arrays, weight)
+    )(frames, places, query, key, value, grad.reshape(clips * rows, width), weight)
 
 
 def shards(query_rows, key_rows, value_rows, out_grad, out_weight, frame_count, pos_count):
     clips, _, places, width = query_rows.shape
     n = lax.axis_size("seq")
     part = places // n
-    moved = exchange(
-        to_positions_kernel,
-        n,
-        (query_rows, key_rows, value_rows, out_grad),
-        (clips, n, part, width),
-        0,
+    moved = to_positions(
+        n, (query_rows, key_rows, value_rows, out_grad), (clips, n, part, width)
     )
     moved = [m.reshape(clips, n * part, width) for m in moved]
-    *results, partial_term = compute(moved, out_weight, frame_count, pos_count, part)
+    *results, term = compute(moved, out_weight, frame_count, pos_count, part)
     results = [r.reshape(clips, n, part, width) for r in results]
-    grad_weight = lax.psum_scatter(partial_term, "seq", scatter_dimension=0, tiled=True)
-    grad_weight = lax.psum(grad_weight, "rep")
-    back = exchange(to_frames_kernel, n, results, (clips, 1, places, width), 1)
-    return (*back, grad_weight)
+    return tuple(to_frames(n, results, term, (clips, 1, places, width)))
 
 
 def solution(mesh):

time: 350 us -> 192 us (0.55)
  waiting for transfers between devices: 173 us -> 0 us
  Pallas kernels: 154 us -> 183 us
  between operations: 14.1 us -> 0.67 us
    unnamed x3 -> x0, waiting for transfers between devices: 94.2 us -> none
    psum x1 -> x0, waiting for transfers between devices: 78.7 us -> none  [shards(): grad_weight = lax.psum(grad_weight, 'rep')]
    pallas_call x2, Pallas kernels: 118 us -> 147 us  [the longest x1 89.5 us: to_frames(): pl.pallas_call(functools.partial(to_frames_kernel, n), out_shape=[jax.Sha...]
  transfers between devices with their start and end apart: 2 -> 0, of which waited for: 2 -> 0; matrix products, arithmetic and copies ran while one was open for 0% -> 0% of each run, Pallas kernels for 17% -> 0%
where the time goes in v2:
time: 192 us
  Pallas kernels  183 us (95%)
  local copies, waits for them, and re-layouts  7.75 us (4%)
    pallas_call x1, Pallas kernels, to_frames(): pl.pallas_call(functools.partial(to_frames_kernel, n), out_shape=[jax.Sha...  89.5 us
    pallas_call x1, Pallas kernels, to_positions(): pl.pallas_call(functools.partial(to_positions_kernel, n), out_shape=[jax....  57.9 us
    pallas_call x1, Pallas kernels, compute(): pl.pallas_call(functools.partial(compute_kernel, part), grid=(clips,), ou...  36 us
    unnamed x13, local copies, waits for them, and re-layouts  7.75 us

profile of v2, /device:TPU:24, one launch (start us, length us, event | category | flops | bytes accessed | tf_op | source)
XLA Modules:
  0.0 191.8 jit_solution(17529798268180608308)
XLA Ops:
  0.6 57.9 %shard_map.110 = (bf16[2,16,16,1152]{3,2,1,0:T(8,128)(2,1)}, bf16[2,16,16,1152]{3,2,1,0:T(8,128)(2,1)}, bf16[2,16,16,1152]{3,2,1,0:T(8,128)(2,1)}, bf16[2,16,16,1152]{3,2,1,0:T(8,128)(2,1)}) custom-call(bf16[2,1,256,1152]{3,2,1,0:T(8,128)(2,1)} %refs_0_.1, bf16[2,1,256,1152]{3,2,1,0:T(8,128)(2,1)} %refs_1_.1, bf16[2,1,256,1152]{3,2,1,0:T(8,128)(2,1)} %refs_2_.1, ...), custom_call_target="tpu_custom_call" | custom-call | tf_op jit(solution)/shard_map/pallas_call | solution.py:285
  58.5 36.0 %shard_map.111 = (bf16[2,256,1152]{2,1,0:T(8,128)(2,1)}, bf16[2,256,1152]{2,1,0:T(8,128)(2,1)}, bf16[2,256,1152]{2,1,0:T(8,128)(2,1)}, bf16[2,256,1152]{2,1,0:T(8,128)(2,1)}, f32[2,8,9,8,1152]{4,3,2,1,0:T(8,128)}) custom-call(s32[2]{0:T(128)} %frames.1, s32[2]{0:T(128)} %places.1, bf16[2,256,1152]{2,1,0:T(8,128)(2,1)} %bitcast.12, ...), custom_call_target="tpu_custom_call" | custom-call | tf_op jit(solution)/shard_map/pallas_call | solution.py:426
  94.5 89.5 %shard_map.112 = (bf16[2,1,256,1152]{3,2,1,0:T(8,128)(2,1)}, bf16[2,1,256,1152]{3,2,1,0:T(8,128)(2,1)}, bf16[2,1,256,1152]{3,2,1,0:T(8,128)(2,1)}, bf16[2,1,256,1152]{3,2,1,0:T(8,128)(2,1)}, f32[72,1152]{1,0:T(8,128)}) custom-call(bf16[2,16,16,1152]{3,2,1,0:T(8,128)(2,1)} %bitcast.8, bf16[2,16,16,1152]{3,2,1,0:T(8,128)(2,1)} %bitcast.9, ...), custom_call_target="tpu_custom_call" | custom-call | tf_op jit(solution)/shard_map/pallas_call | solution.py:298
  184.0 0.0 copy-start.2
  184.0 2.5 %copy.17 = bf16[2,1,256,1152]{3,2,1,0:T(8,128)(2,1)} copy(bf16[2,1,256,1152]{3,2,1,0:T(8,128)(2,1)} %get-tuple-element.28) | data formatting | bytes 2359296
  186.5 0.0 copy-done.2
  186.5 0.0 copy-start.1
  186.5 1.0 copy.18
  187.5 0.7 copy-done.1
  188.2 0.0 copy-start
  188.2 1.0 copy.19
  189.2 0.7 copy-done
  189.9 0.0 copy-start.3
  189.9 1.0 copy.20
  190.9 0.1 copy-done.3
  191.0 0.7 copy.21
Async XLA Ops:
  184.0 2.5 %copy-start.2 = (bf16[2,1,256,1152]{3,2,1,0:T(8,128)(2,1)S(1)}, bf16[2,1,256,1152]{3,2,1,0:T(8,128)(2,1)}, u32[]{:S(2)}) copy-start(bf16[2,1,256,1152]{3,2,1,0:T(8,128)(2,1)} %get-tuple-element.29) | copy-start | bytes 3538948
  186.5 1.7 copy-start.1
  188.2 1.7 copy-start
  189.9 1.2 copy-start.3

commit v3 on v2

v3 whole, which is shorter than its diff:
```python
import functools
import math

import jax
import jax.numpy as jnp
from jax import lax
from jax.experimental import pallas as pl
from jax.experimental.pallas import tpu as pltpu
from jax.sharding import PartitionSpec as P

HEADS = 16
RING = 8
SLABS = 9
TOGETHER = 4
SUB = 3
MESH = pl.DeviceIdType.MESH
VMEM_BYTES = 56 << 20


def greet(peers):
    barrier = pltpu.get_barrier_semaphore()
    for first, count, peer_of in peers:

        def signal(j, carry):
            pl.semaphore_signal(barrier, inc=1, device_id=peer_of(j), device_id_type=MESH)
            return carry

        lax.fori_loop(first, first + count, signal, 0)
    pl.semaphore_wait(barrier, sum(count for _, count, _ in peers))


def row_peers(n):
    s, r = lax.axis_index("seq"), lax.axis_index("rep")
    return (1, n - 1, lambda j: (lax.rem(s + j, n), r))


def slab_place(slab):
    block, i = slab // SLABS, slab % SLABS
    core, chip = block % 2, block // 2
    return (core, i, chip) if i < RING else (core, chip, RING)


class WeightSum:
    def __init__(self, term, out, half, ring, plane, last, sems):
        self.term, self.out, self.half, self.ring, self.plane, self.last = (
            term, out, half, ring, plane, last,
        )
        (self.half_sems, self.ring_send, self.ring_recv, self.plane_sems, self.z_sems) = sems
        self.s, self.r = lax.axis_index("seq"), lax.axis_index("rep")
        self.core, self.chip = lax.rem(self.s, 2), lax.div(self.s, 2)
        self.z, self.low = lax.rem(self.r, RING), lax.div(self.r, RING)

    def peers(self):
        s, r, core, z, low = self.s, self.r, self.core, self.z, self.low
        return [
            (0, RING, lambda j: (2 * j + core, (1 - low) * RING + z)),
            (1, RING - 1, lambda j: (s, low * RING + lax.rem(z + j, RING))),
        ]

    def half_copy(self):
        return pltpu.make_async_remote_copy(
            src_ref=self.term.at[1 - self.core],
            dst_ref=self.half,
            send_sem=self.half_sems.at[0],
            recv_sem=self.half_sems.at[1],
            device_id=(self.s + 1 - 2 * self.core, self.r),
            device_id_type=MESH,
        )

    def add_half(self):
        self.half_copy().wait()

        def add(j, carry):
            self.half[j] += self.term[self.core, j]
            return carry

        lax.fori_loop(0, RING, add, 0)

    def piece(self, t):
        way = 1 - 2 * self.core
        return lax.rem(self.z - way * (t + 1) + 2 * RING, RING)

    def ring_copy(self, t, u):
        way = 1 - 2 * self.core
        slots = pl.ds(u * SUB, SUB)
        return pltpu.make_async_remote_copy(
            src_ref=self.half.at[self.piece(0), slots] if t == 0 else self.ring.at[t - 1, slots],
            dst_ref=self.ring.at[t, slots],
            send_sem=self.ring_send.at[t, u],
            recv_sem=self.ring_recv.at[t, u],
            device_id=(self.s, self.low * RING + lax.rem(self.z + way + RING, RING)),
            device_id_type=MESH,
        )

    def ring_start(self):
        for u in range(SLABS // SUB):
            self.ring_copy(0, u).start()

    def ring_step(self, t):
        for u in range(SLABS // SUB):
            slots = pl.ds(u * SUB, SUB)
            self.ring_copy(t, u).wait_recv()
            self.ring[t, slots] += self.half[self.piece(t + 1), slots]
            if t + 1 < RING - 1:
                self.ring_copy(t + 1, u).start()

    def spread(self, start):
        held, me = self.ring.at[RING - 2], self.low * RING + self.chip

        def each(j, carry):
            chip, low = lax.rem(j, RING), lax.div(j, RING)
            self.plane_copy(held.at[chip], self.plane.at[0, me], 0, 2 * chip + self.core, low, start)
            return carry

        lax.fori_loop(0, 2 * RING, each, 0)
        for low in range(2):
            self.plane_copy(held.at[RING], self.plane.at[1, me], 1, 2 * self.z + self.core, low, start)

    def plane_copy(self, src, dst, k, s, low, start):
        is_self = (s == self.s) & (low == self.low)

        @pl.when(jnp.logical_not(is_self))
        def _():
            copy = pltpu.make_async_remote_copy(
                src_ref=src,
                dst_ref=dst,
                send_sem=self.plane_sems.at[0, k],
                recv_sem=self.plane_sems.at[1, k],
                device_id=(s, low * RING + self.z),
                device_id_type=MESH,
            )
            if start:
                copy.start()
            else:
                copy.wait_send()

        if start:

            @pl.when(is_self)
            def _():
                self.plane[k, self.low * RING + self.chip] = self.ring[
                    RING - 2, self.chip if k == 0 else RING
                ]

    def z_copy(self, k, j):
        rows = pl.ds(pl.multiple_of(self.z * 8, 8) if k == 0 else RING * 8, 8)
        return pltpu.make_async_remote_copy(
            src_ref=self.last.at[k],
            dst_ref=self.out.at[rows],
            send_sem=self.z_sems.at[0, k],
            recv_sem=self.z_sems.at[1, k],
            device_id=(self.s, self.low * RING + lax.rem(self.z + j, RING)),
            device_id_type=MESH,
        )

    def to_all_z(self, k, start):
        def each(j, carry):
            copy = self.z_copy(k, j)
            if start:
                copy.start()
            else:
                copy.wait_send()
            return carry

        lax.fori_loop(1, RING, each, 0)

    def gather(self):
        for k in range(2):

            @pl.when((self.chip == self.z) | (k == 0))
            def _():
                whole = self.plane.at[k, pl.ds(0, 2 * RING - 1)]
                pltpu.make_async_copy(whole, whole, self.plane_sems.at[1, k]).wait()
                total = self.plane[k, 0]
                for i in range(1, 2 * RING):
                    total = total + self.plane[k, i]
                self.last[k] = total
                self.to_all_z(k, True)
                rows = pl.ds(pl.multiple_of(self.z * 8, 8) if k == 0 else RING * 8, 8)
                self.out[rows] = total

    def finish(self):
        whole = self.plane.at[0, pl.ds(0, RING - 1)]
        pltpu.make_async_copy(whole, whole, self.z_sems.at[1, 0]).wait()
        self.to_all_z(0, False)

        @pl.when(self.chip == self.z)
        def _():
            self.to_all_z(1, False)

        @pl.when(self.chip != self.z)
        def _():
            one = self.plane.at[1, 0]
            pltpu.make_async_copy(one, one, self.z_sems.at[1, 1]).wait()

        self.spread(False)
        for t in range(RING - 1):
            for u in range(SLABS // SUB):
                self.ring_copy(t, u).wait_send()


def columns_of(width):
    step = 384 if width % 384 == 0 else width
    return [pl.ds(i, step) for i in range(0, width, step)]


def dot(a, b, over):
    return lax.dot_general(a, b, ((over[:1], over[1:]), ((), ())), preferred_element_type=jnp.float32)


class Attention:
    def __init__(self, part, frames, places, weight, arrived, results, scratch):
        self.part, self.frames, self.places, self.weight = part, frames, places, weight
        self.query, self.key, self.value, self.grad = arrived
        self.projected, self.grad_query, self.grad_key, self.grad_value = results
        self.cot, self.attn, self.bias, self.probs = scratch
        self.width = weight.shape[0]
        self.head_dim = self.width // HEADS
        self.count = self.bias.shape[0]

    def rows(self, c):
        return pl.ds(c * self.count, self.count)

    def live(self, c):
        row = lax.broadcasted_iota(jnp.int32, (self.count, 1), 0)
        place = lax.axis_index("seq") * self.part + row % self.part
        return (row // self.part < self.frames[c]) & (place < self.places[c])

    def window(self, h):
        low = jnp.minimum((h * self.head_dim) // 128 * 128, self.width - 256)
        lane = lax.broadcasted_iota(jnp.int32, (self.count, 256), 1) + low
        inside = (lane >= h * self.head_dim) & (lane < (h + 1) * self.head_dim)
        return pl.ds(pl.multiple_of(low, 128), 256), inside

    def forward(self, c):
        rows, count, part = self.rows(c), self.count, self.part
        key_row = lax.broadcasted_iota(jnp.int32, (count, count), 0)
        query_row = lax.broadcasted_iota(jnp.int32, (count, count), 1)
        allowed = (key_row % part == query_row % part) & (key_row // part < self.frames[c])
        self.bias[...] = jnp.where(allowed, 0.0, -1e30)
        live = self.live(c)
        scale = math.log2(math.e) / math.sqrt(self.head_dim)

        def head(h, carry):
            window, inside = self.window(h)
            query = jnp.where(inside, self.query[rows, window], 0.0).astype(jnp.bfloat16)
            scores = dot(self.key[rows, window], query, (1, 1)) + self.bias[...]
            highest = jnp.max(scores, axis=0, keepdims=True)
            expo = jnp.exp2((scores - highest) * scale)
            weights = expo * (1.0 / jnp.sum(expo, axis=0, keepdims=True))
            self.probs[h] = weights
            mixed = dot(weights.astype(jnp.bfloat16), self.value[rows, window], (0, 0))
            mixed = jnp.where(live, mixed, 0.0).astype(jnp.bfloat16)
            self.attn[rows, window] = jnp.where(inside, mixed, self.attn[rows, window])
            return carry

        lax.fori_loop(0, HEADS, head, 0)

    def cotangent(self, c):
        live = self.live(c)
        for cols in columns_of(self.width):
            wide = dot(self.grad[self.rows(c), :], self.weight[:, cols], (1, 0))
            self.cot[:, cols] = jnp.where(live, wide, 0.0).astype(jnp.bfloat16)

    def project(self, c):
        for cols in columns_of(self.width):
            wide = dot(self.attn[self.rows(c), :], self.weight[cols, :], (1, 1))
            self.projected[self.rows(c), cols] = wide.astype(jnp.bfloat16)

    def backward(self, c, first, past):
        rows = self.rows(c)
        inv_root = 1.0 / math.sqrt(self.head_dim)

        def head(h, carry):
            window, inside = self.window(h)
            key = self.key[rows, window]
            query = jnp.where(inside, self.query[rows, window], 0.0).astype(jnp.bfloat16)
            cot = jnp.where(inside, self.cot[:, window], 0.0).astype(jnp.bfloat16)
            weights = self.probs[h]

            def keep(target, found):
                found = found.astype(jnp.bfloat16)
                target[rows, window] = jnp.where(inside, found, target[rows, window])

            keep(self.grad_value, dot(weights.astype(jnp.bfloat16), cot, (1, 0)))
            grad_attn = dot(self.value[rows, window], cot, (1, 1))
            delta = jnp.sum(weights * grad_attn, axis=0, keepdims=True)
            grad_score = weights * (grad_attn - delta) * inv_root
            coarse = grad_score.astype(jnp.bfloat16)
            fine = (grad_score - coarse.astype(jnp.float32)).astype(jnp.bfloat16)
            keep(self.grad_query, dot(coarse, key, (0, 0)) + dot(fine, key, (0, 0)))
            keep(self.grad_key, dot(coarse, query, (1, 0)) + dot(fine, query, (1, 0)))
            return carry

        lax.fori_loop(first, past, head, 0)

    def weight_term(self, term):
        for cols in columns_of(self.width):
            found = dot(self.grad[:, cols], self.attn[...], (0, 0))
            for k in range(cols.size // 8):
                term[slab_place(cols.start // 8 + k)] = found[8 * k : 8 * k + 8]


class Exchange:
    def __init__(self, n, clips, part, sems):
        self.n, self.clips, self.part = n, clips, part
        self.send, self.recv, self.local = sems
        self.me, self.rep = lax.axis_index("seq"), lax.axis_index("rep")

    def start(self, c, a, here, place):
        pltpu.make_async_copy(here(self.me), place, self.local.at[c, a]).start()

        def push(j, carry):
            peer = lax.rem(self.me + j, self.n)
            pltpu.make_async_remote_copy(
                src_ref=here(peer),
                dst_ref=place,
                send_sem=self.send.at[c, a],
                recv_sem=self.recv.at[c, a],
                device_id=(peer, self.rep),
                device_id_type=MESH,
            ).start()
            return carry

        lax.fori_loop(1, self.n, push, 0)

    def tile(self, array, c, owner):
        return array.at[pl.ds(pl.multiple_of((c * self.n + owner) * self.part, self.part), self.part)]

    def strip(self, array, c, owner):
        return array.at[c, 0, pl.ds(pl.multiple_of(owner * self.part, self.part), self.part)]

    def bring(self, c, a, source, target):
        self.start(c, a, lambda peer: self.strip(source, c, peer), self.tile(target, c, self.me))

    def give(self, c, a, source, target):
        self.start(c, a, lambda peer: self.tile(source, c, peer), self.strip(target, c, self.me))

    def wait(self, sem, count, array):
        some = array.at[pl.ds(0, count * self.part)]
        pltpu.make_async_copy(some, some, sem).wait()

    def arrived(self, c, a, array):
        self.wait(self.local.at[c, a], 1, array)
        self.wait(self.recv.at[c, a], self.n - 1, array)

    def left(self, c, a, array):
        self.wait(self.send.at[c, a], self.n - 1, array)


def fused_kernel(n, part, frames, places, *refs):
    sources, weight, targets, out = refs[:4], refs[4], refs[5:9], refs[9]
    arrived, results, scratch = refs[10:14], refs[14:18], refs[18:22]
    term, half, ring, plane, last = refs[22:27]
    clips = sources[0].shape[0]
    inward, outward = Exchange(n, clips, part, refs[27:30]), Exchange(n, clips, part, refs[30:33])
    weight_sum = WeightSum(term, out, half, ring, plane, last, refs[33:])
    work = Attention(part, frames, places, weight, arrived, results, scratch)
    greet([row_peers(n)] + weight_sum.peers())
    for c in range(clips):
        for a in range(4):
            inward.bring(c, a, sources[a], arrived[a])

    def give(c, a):
        outward.give(c, a, results[a], targets[a])

    end = clips - 1
    for c in range(clips):
        for a in range(3):
            inward.arrived(c, a, arrived[a])
        work.forward(c)
        inward.arrived(c, 3, arrived[3])
        if c < end:
            work.cotangent(c)
            work.backward(c, 0, HEADS)
            work.project(c)
    work.weight_term(term)
    weight_sum.half_copy().start()
    for c in range(end):
        for a in range(4):
            give(c, a)
    work.project(end)
    give(end, 0)
    work.cotangent(end)
    weight_sum.add_half()
    weight_sum.ring_start()
    for t in range(RING - 1):
        if t * TOGETHER < HEADS:
            work.backward(end, t * TOGETHER, (t + 1) * TOGETHER)
            if (t + 1) * TOGETHER == HEADS:
                for a in range(1, 4):
                    give(end, a)
        weight_sum.ring_step(t)
    weight_sum.spread(True)
    weight_sum.gather()
    weight_sum.finish()
    for c in range(clips):
        for a in range(4):
            inward.left(c, a, arrived[a])
            outward.arrived(c, a, results[a])
            outward.left(c, a, results[a])


def fused(n, arrays, weight, frames, places):
    clips, _, all_places, width = arrays[0].shape
    part = all_places // n
    rows = n * part
    dma = pltpu.SemaphoreType.DMA
    smem, vmem, anywhere = (
        pl.BlockSpec(memory_space=space) for space in (pltpu.SMEM, pltpu.VMEM, pl.ANY)
    )
    return pl.pallas_call(
        functools.partial(fused_kernel, n, part),
        out_shape=[jax.ShapeDtypeStruct(arrays[0].shape, jnp.bfloat16)] * 4
        + [jax.ShapeDtypeStruct((SLABS * 8, width), jnp.float32)],
        in_specs=[smem, smem] + [anywhere] * 4 + [vmem],
        out_specs=[anywhere] * 4 + [vmem],
        scratch_shapes=[pltpu.VMEM((clips * rows, width), jnp.bfloat16)] * 8
        + [
            pltpu.VMEM((rows, width), jnp.bfloat16),
            pltpu.VMEM((clips * rows, width), jnp.bfloat16),
            pltpu.VMEM((rows, rows), jnp.float32),
            pltpu.VMEM((HEADS, rows, rows), jnp.float32),
            pltpu.VMEM((2, RING, SLABS, 8, width), jnp.float32),
            pltpu.VMEM((RING, SLABS, 8, width), jnp.float32),
            pltpu.VMEM((RING - 1, SLABS, 8, width), jnp.float32),
            pltpu.VMEM((2, 2 * RING, 8, width), jnp.float32),
            pltpu.VMEM((2, 8, width), jnp.float32),
        ]
        + [dma((clips, 4))] * 6
        + [dma((2,)), dma((RING - 1, SLABS // SUB)), dma((RING - 1, SLABS // SUB)), dma((2, 2)), dma((2, 2))],
        compiler_params=pltpu.CompilerParams(
            collective_id=0, has_side_effects=True, vmem_limit_bytes=VMEM_BYTES
        ),
    )(frames, places, *arrays, weight)


def deliver_kernel(*refs):
    count = (len(refs) - 2) // 3
    sources, targets, held = refs[:count], refs[count : 2 * count], refs[2 * count : 3 * count]
    fetch = [pltpu.make_async_copy(sources[i], held[i], refs[-2].at[i]) for i in range(count)]
    store = [pltpu.make_async_copy(held[i], targets[i], refs[-1].at[i]) for i in range(count)]
    for copy in fetch:
        copy.start()
    for i in range(count):
        fetch[i].wait()
        store[i].start()
    for copy in store:
        copy.wait()


def deliver(arrays):
    count = len(arrays)
    return pl.pallas_call(
        deliver_kernel,
        out_shape=[jax.ShapeDtypeStruct(a.shape, a.dtype) for a in arrays],
        in_specs=[pl.BlockSpec(memory_space=pl.ANY)] * count,
        out_specs=[pl.BlockSpec(memory_space=pl.ANY)] * count,
        scratch_shapes=[pltpu.VMEM(a.shape, a.dtype) for a in arrays]
        + [pltpu.SemaphoreType.DMA((count,))] * 2,
        compiler_params=pltpu.CompilerParams(vmem_limit_bytes=VMEM_BYTES),
    )(*arrays)


def shards(query_rows, key_rows, value_rows, out_grad, out_weight, frame_count, pos_count):
    n = lax.axis_size("seq")
    arrays = (query_rows, key_rows, value_rows, out_grad)
    return tuple(deliver(fused(n, arrays, out_weight, frame_count, pos_count)))


def solution(mesh):
    rows = P("rep", "seq", None, None)
    return jax.shard_map(
        shards,
        mesh=mesh,
        in_specs=(rows, rows, rows, rows, P(), P("rep"), P("rep")),
        out_specs=(rows, rows, rows, rows, P("seq", None)),
        check_vma=False,
    )
```

time: 192 us -> 153 us (0.80)
  Pallas kernels: 183 us -> 152 us
  local copies, waits for them, and re-layouts: 7.75 us -> 0 us
    pallas_call x3 -> x2, Pallas kernels: 183 us -> 152 us  [the longest x1 149 us: fused(): pl.pallas_call(functools.partial(fused_kernel, n, part), out_shape=[jax.S...]
    unnamed x13 -> x0, local copies, waits for them, and re-layouts: 7.75 us -> none
where the time goes in v3:
time: 153 us
  Pallas kernels  152 us (99%)
    pallas_call x1, Pallas kernels, fused(): pl.pallas_call(functools.partial(fused_kernel, n, part), out_shape=[jax.S...  149 us
    pallas_call x1, Pallas kernels, deliver(): pl.pallas_call(deliver_kernel, out_shape=[jax.ShapeDtypeStruct(a.shape, a...  3.87 us

profile of v3, /device:TPU:24, one launch (start us, length us, event | category | flops | bytes accessed | tf_op | source)
XLA Modules:
  0.0 153.1 jit_solution(15013976814451449851)
XLA Ops:
  0.6 148.5 %shard_map.110 = (bf16[2,1,256,1152]{3,2,1,0:T(8,128)(2,1)}, bf16[2,1,256,1152]{3,2,1,0:T(8,128)(2,1)}, bf16[2,1,256,1152]{3,2,1,0:T(8,128)(2,1)}, bf16[2,1,256,1152]{3,2,1,0:T(8,128)(2,1)}, f32[72,1152]{1,0:T(8,128)}) custom-call(s32[2]{0:T(128)} %frames.1, s32[2]{0:T(128)} %places.1, bf16[2,1,256,1152]{3,2,1,0:T(8,128)(2,1)} %refs_0_.1, ...), custom_call_target="tpu_custom_call" | custom-call | tf_op jit(solution)/shard_map/pallas_call | solution.py:412
  149.2 3.9 %shard_map.111 = (bf16[2,1,256,1152]{3,2,1,0:T(8,128)(2,1)}, bf16[2,1,256,1152]{3,2,1,0:T(8,128)(2,1)}, bf16[2,1,256,1152]{3,2,1,0:T(8,128)(2,1)}, bf16[2,1,256,1152]{3,2,1,0:T(8,128)(2,1)}, f32[72,1152]{1,0:T(8,128)}) custom-call(bf16[2,1,256,1152]{3,2,1,0:T(8,128)(2,1)} %get-tuple-element.10.refs_0_, bf16[2,1,256,1152]{3,2,1,0:T(8,128)(2,1)} %get-tuple-element.11.refs_1_, ...), custom_call_target="tpu_custom_call" | custom-call | tf_op jit(solution)/shard_map/pallas_call | solution.py:454

commit v4 on v3

--- a/solution.py
+++ b/solution.py
@@ -11,7 +11,9 @@
 HEADS = 16
 RING = 8
 SLABS = 9
-TOGETHER = 4
+TOGETHER = 2
+BATCH = 3
+HALVES = (pl.ds(0, 640), pl.ds(640, 512))
 SUB = 3
 MESH = pl.DeviceIdType.MESH
 VMEM_BYTES = 56 << 20
@@ -52,9 +54,11 @@
 
     def peers(self):
         s, r, core, z, low = self.s, self.r, self.core, self.z, self.low
+        other = (1 - low) * RING
         return [
-            (0, RING, lambda j: (2 * j + core, (1 - low) * RING + z)),
+            (0, RING, lambda j: (2 * j + core, other + z)),
             (1, RING - 1, lambda j: (s, low * RING + lax.rem(z + j, RING))),
+            (1, RING - 1, lambda j: (s, other + lax.rem(z + j, RING))),
         ]
 
     def half_copy(self):
@@ -96,34 +100,34 @@
         for u in range(SLABS // SUB):
             self.ring_copy(0, u).start()
 
-    def ring_step(self, t):
-        for u in range(SLABS // SUB):
-            slots = pl.ds(u * SUB, SUB)
-            self.ring_copy(t, u).wait_recv()
-            self.ring[t, slots] += self.half[self.piece(t + 1), slots]
-            if t + 1 < RING - 1:
-                self.ring_copy(t + 1, u).start()
+    def ring_step(self, t, u):
+        slots = pl.ds(u * SUB, SUB)
+        self.ring_copy(t, u).wait_recv()
+        self.ring[t, slots] += self.half[self.piece(t + 1), slots]
+        if t + 1 < RING - 1:
+            self.ring_copy(t + 1, u).start()
 
     def spread(self, start):
-        held, me = self.ring.at[RING - 2], self.low * RING + self.chip
-
-        def each(j, carry):
-            chip, low = lax.rem(j, RING), lax.div(j, RING)
-            self.plane_copy(held.at[chip], self.plane.at[0, me], 0, 2 * chip + self.core, low, start)
-            return carry
-
-        lax.fori_loop(0, 2 * RING, each, 0)
+        me = self.low * RING + self.chip
         for low in range(2):
-            self.plane_copy(held.at[RING], self.plane.at[1, me], 1, 2 * self.z + self.core, low, start)
-
-    def plane_copy(self, src, dst, k, s, low, start):
+
+            def each(chip, carry):
+                self.plane_copy(chip, 0, me, 2 * chip + self.core, low, start)
+                return carry
+
+            lax.fori_loop(0, RING, each, 0)
+            self.plane_copy(RING, 1, me, 2 * self.z + self.core, low, start)
+
+    def plane_copy(self, slot, k, me, s, low, start):
         is_self = (s == self.s) & (low == self.low)
+        cols = HALVES[low]
+        held = self.ring.at[RING - 2, slot, :, cols]
 
         @pl.when(jnp.logical_not(is_self))
         def _():
             copy = pltpu.make_async_remote_copy(
-                src_ref=src,
-                dst_ref=dst,
+                src_ref=held,
+                dst_ref=self.plane.at[k, me, :, pl.ds(0, cols.size)],
                 send_sem=self.plane_sems.at[0, k],
                 recv_sem=self.plane_sems.at[1, k],
                 device_id=(s, low * RING + self.z),
@@ -138,60 +142,69 @@
 
             @pl.when(is_self)
             def _():
-                self.plane[k, self.low * RING + self.chip] = self.ring[
-                    RING - 2, self.chip if k == 0 else RING
-                ]
-
-    def z_copy(self, k, j):
-        rows = pl.ds(pl.multiple_of(self.z * 8, 8) if k == 0 else RING * 8, 8)
-        return pltpu.make_async_remote_copy(
-            src_ref=self.last.at[k],
-            dst_ref=self.out.at[rows],
-            send_sem=self.z_sems.at[0, k],
-            recv_sem=self.z_sems.at[1, k],
-            device_id=(self.s, self.low * RING + lax.rem(self.z + j, RING)),
-            device_id_type=MESH,
-        )
-
-    def to_all_z(self, k, start):
+                self.plane[k, me, :, pl.ds(0, cols.size)] = self.ring[RING - 2, slot, :, cols]
+
+    def own_rows(self, k):
+        return pl.ds(pl.multiple_of(self.z * 8, 8) if k == 0 else RING * 8, 8)
+
+    def to_all(self, k, low, start):
+        cols = HALVES[low]
+
         def each(j, carry):
-            copy = self.z_copy(k, j)
+            copy = pltpu.make_async_remote_copy(
+                src_ref=self.last.at[k, :, pl.ds(0, cols.size)],
+                dst_ref=self.out.at[self.own_rows(k), cols],
+                send_sem=self.z_sems.at[0, k],
+                recv_sem=self.z_sems.at[1 + low, k],
+                device_id=(self.s, lax.rem(self.r + j, 2 * RING)),
+                device_id_type=MESH,
+            )
             if start:
                 copy.start()
             else:
                 copy.wait_send()
             return carry
 
-        lax.fori_loop(1, RING, each, 0)
+        lax.fori_loop(1, 2 * RING, each, 0)
 
     def gather(self):
         for k in range(2):
-
-            @pl.when((self.chip == self.z) | (k == 0))
+            for low in range(2):
+
+                @pl.when((self.low == low) & ((self.chip == self.z) | (k == 0)))
+                def _():
+                    cols = HALVES[low]
+                    some = pl.ds(0, cols.size)
+                    whole = self.plane.at[k, pl.ds(0, 2 * RING - 1), :, some]
+                    pltpu.make_async_copy(whole, whole, self.plane_sems.at[1, k]).wait()
+                    total = self.plane[k, 0, :, some]
+                    for i in range(1, 2 * RING):
+                        total = total + self.plane[k, i, :, some]
+                    self.last[k, :, some] = total
+                    self.to_all(k, low, True)
+                    self.out[self.own_rows(k), cols] = total
+
+    def finish(self):
+        for low in range(2):
+            mine = self.low == low
+            some = pl.ds(0, HALVES[low].size)
+            for count, is_count in ((RING - 1, mine), (RING, jnp.logical_not(mine))):
+
+                @pl.when(is_count)
+                def _():
+                    whole = self.plane.at[0, pl.ds(0, count), :, some]
+                    pltpu.make_async_copy(whole, whole, self.z_sems.at[1 + low, 0]).wait()
+
+            @pl.when(jnp.logical_not(mine & (self.chip == self.z)))
             def _():
-                whole = self.plane.at[k, pl.ds(0, 2 * RING - 1)]
-                pltpu.make_async_copy(whole, whole, self.plane_sems.at[1, k]).wait()
-                total = self.plane[k, 0]
-                for i in range(1, 2 * RING):
-                    total = total + self.plane[k, i]
-                self.last[k] = total
-                self.to_all_z(k, True)
-                rows = pl.ds(pl.multiple_of(self.z * 8, 8) if k == 0 else RING * 8, 8)
-                self.out[rows] = total
-
-    def finish(self):
-        whole = self.plane.at[0, pl.ds(0, RING - 1)]
-        pltpu.make_async_copy(whole, whole, self.z_sems.at[1, 0]).wait()
-        self.to_all_z(0, False)
-
-        @pl.when(self.chip == self.z)
-        def _():
-            self.to_all_z(1, False)
-
-        @pl.when(self.chip != self.z)
-        def _():
-            one = self.plane.at[1, 0]
-            pltpu.make_async_copy(one, one, self.z_sems.at[1, 1]).wait()
+                one = self.plane.at[1, 0, :, some]
+                pltpu.make_async_copy(one, one, self.z_sems.at[1 + low, 1]).wait()
+
+            for k in range(2):
+
+                @pl.when(mine & ((self.chip == self.z) | (k == 0)))
+                def _():
+                    self.to_all(k, low, False)
 
         self.spread(False)
         for t in range(RING - 1):
@@ -307,8 +320,9 @@
         self.send, self.recv, self.local = sems
         self.me, self.rep = lax.axis_index("seq"), lax.axis_index("rep")
 
-    def start(self, c, a, here, place):
-        pltpu.make_async_copy(here(self.me), place, self.local.at[c, a]).start()
+    def start(self, c, a, here, place, first, past):
+        if first == 0:
+            pltpu.make_async_copy(here(self.me), place, self.local.at[c, a]).start()
 
         def push(j, carry):
             peer = lax.rem(self.me + j, self.n)
@@ -322,7 +336,7 @@
             ).start()
             return carry
 
-        lax.fori_loop(1, self.n, push, 0)
+        lax.fori_loop(max(first, 1), past, push, 0)
 
     def tile(self, array, c, owner):
         return array.at[pl.ds(pl.multiple_of((c * self.n + owner) * self.part, self.part), self.part)]
@@ -331,10 +345,11 @@
         return array.at[c, 0, pl.ds(pl.multiple_of(owner * self.part, self.part), self.part)]
 
     def bring(self, c, a, source, target):
-        self.start(c, a, lambda peer: self.strip(source, c, peer), self.tile(target, c, self.me))
-
-    def give(self, c, a, source, target):
-        self.start(c, a, lambda peer: self.tile(source, c, peer), self.strip(target, c, self.me))
+        self.start(c, a, lambda peer: self.strip(source, c, peer), self.tile(target, c, self.me), 0, self.n)
+
+    def give(self, c, a, source, target, first, past):
+        place = self.strip(target, c, self.me)
+        self.start(c, a, lambda peer: self.tile(source, c, peer), place, first, past)
 
     def wait(self, sem, count, array):
         some = array.at[pl.ds(0, count * self.part)]
@@ -349,50 +364,68 @@
 
 
 def fused_kernel(n, part, frames, places, *refs):
-    sources, weight, targets, out = refs[:4], refs[4], refs[5:9], refs[9]
+    sources, weight_hbm, targets, out = refs[:4], refs[4], refs[5:9], refs[9]
     arrived, results, scratch = refs[10:14], refs[14:18], refs[18:22]
-    term, half, ring, plane, last = refs[22:27]
+    term, half, ring, plane, last, weight, weight_sem = refs[22:29]
     clips = sources[0].shape[0]
-    inward, outward = Exchange(n, clips, part, refs[27:30]), Exchange(n, clips, part, refs[30:33])
-    weight_sum = WeightSum(term, out, half, ring, plane, last, refs[33:])
+    inward, outward = Exchange(n, clips, part, refs[29:32]), Exchange(n, clips, part, refs[32:35])
+    weight_sum = WeightSum(term, out, half, ring, plane, last, refs[35:])
     work = Attention(part, frames, places, weight, arrived, results, scratch)
+    fetch = pltpu.make_async_copy(weight_hbm, weight, weight_sem)
+    fetch.start()
     greet([row_peers(n)] + weight_sum.peers())
     for c in range(clips):
         for a in range(4):
             inward.bring(c, a, sources[a], arrived[a])
 
-    def give(c, a):
-        outward.give(c, a, results[a], targets[a])
+    ready = []
+
+    def offer(c, arrays):
+        ready.extend((c, a, first) for a in arrays for first in range(0, n, BATCH))
+
+    def give(batches):
+        for c, a, first in ready[:batches]:
+            outward.give(c, a, results[a], targets[a], first, min(first + BATCH, n))
+        del ready[:batches]
 
     end = clips - 1
     for c in range(clips):
         for a in range(3):
             inward.arrived(c, a, arrived[a])
+        if c == end:
+            give(4)
         work.forward(c)
         inward.arrived(c, 3, arrived[3])
+        if c == 0:
+            fetch.wait()
         if c < end:
             work.cotangent(c)
             work.backward(c, 0, HEADS)
             work.project(c)
+            offer(c, range(4))
+    give(8)
     work.weight_term(term)
     weight_sum.half_copy().start()
-    for c in range(end):
-        for a in range(4):
-            give(c, a)
+    give(6)
     work.project(end)
-    give(end, 0)
+    offer(end, [0])
     work.cotangent(end)
     weight_sum.add_half()
     weight_sum.ring_start()
+    done = 0
     for t in range(RING - 1):
-        if t * TOGETHER < HEADS:
-            work.backward(end, t * TOGETHER, (t + 1) * TOGETHER)
-            if (t + 1) * TOGETHER == HEADS:
-                for a in range(1, 4):
-                    give(end, a)
-        weight_sum.ring_step(t)
+        for u in range(SLABS // SUB):
+            if done < HEADS:
+                work.backward(end, done, done + TOGETHER)
+                done += TOGETHER
+                if done == HEADS:
+                    offer(end, range(1, 4))
+            weight_sum.ring_step(t, u)
+            give(1)
     weight_sum.spread(True)
+    give(3)
     weight_sum.gather()
+    give(len(ready))
     weight_sum.finish()
     for c in range(clips):
         for a in range(4):
@@ -413,7 +446,7 @@
         functools.partial(fused_kernel, n, part),
         out_shape=[jax.ShapeDtypeStruct(arrays[0].shape, jnp.bfloat16)] * 4
         + [jax.ShapeDtypeStruct((SLABS * 8, width), jnp.float32)],
-        in_specs=[smem, smem] + [anywhere] * 4 + [vmem],
+        in_specs=[smem, smem] + [anywhere] * 5,
         out_specs=[anywhere] * 4 + [vmem],
         scratch_shapes=[pltpu.VMEM((clips * rows, width), jnp.bfloat16)] * 8
         + [
@@ -424,11 +457,13 @@
             pltpu.VMEM((2, RING, SLABS, 8, width), jnp.float32),
             pltpu.VMEM((RING, SLABS, 8, width), jnp.float32),
             pltpu.VMEM((RING - 1, SLABS, 8, width), jnp.float32),
-            pltpu.VMEM((2, 2 * RING, 8, width), jnp.float32),
-            pltpu.VMEM((2, 8, width), jnp.float32),
+            pltpu.VMEM((2, 2 * RING, 8, 640), jnp.float32),
+            pltpu.VMEM((2, 8, 640), jnp.float32),
+            pltpu.VMEM((width, width), jnp.bfloat16),
+            dma(()),
         ]
         + [dma((clips, 4))] * 6
-        + [dma((2,)), dma((RING - 1, SLABS // SUB)), dma((RING - 1, SLABS // SUB)), dma((2, 2)), dma((2, 2))],
+        + [dma((2,)), dma((RING - 1, SLABS // SUB)), dma((RING - 1, SLABS // SUB)), dma((2, 2)), dma((3, 2))],
         compiler_params=pltpu.CompilerParams(
             collective_id=0, has_side_effects=True, vmem_limit_bytes=VMEM_BYTES
         ),

time: 153 us -> 138 us (0.902)
  Pallas kernels: 152 us -> 136 us
    pallas_call x1, Pallas kernels: 149 us -> 132 us  [fused(): pl.pallas_call(functools.partial(fused_kernel, n, part), out_shape=[jax.S...]
where the time goes in v4:
time: 138 us; the launch traced here: 137 us
  Pallas kernels  136 us (99%)
    pallas_call x1, Pallas kernels, fused(): pl.pallas_call(functools.partial(fused_kernel, n, part), out_shape=[jax.S...  132 us
    pallas_call x1, Pallas kernels, deliver(): pl.pallas_call(deliver_kernel, out_shape=[jax.ShapeDtypeStruct(a.shape, a...  3.87 us

profile of v4, /device:TPU:24, one launch (start us, length us, event | category | flops | bytes accessed | tf_op | source)
XLA Modules:
  0.0 136.8 jit_solution(6184369550331306870)
XLA Ops:
  0.6 132.3 %shard_map.110 = (bf16[2,1,256,1152]{3,2,1,0:T(8,128)(2,1)}, bf16[2,1,256,1152]{3,2,1,0:T(8,128)(2,1)}, bf16[2,1,256,1152]{3,2,1,0:T(8,128)(2,1)}, bf16[2,1,256,1152]{3,2,1,0:T(8,128)(2,1)}, f32[72,1152]{1,0:T(8,128)}) custom-call(s32[2]{0:T(128)} %frames.1, s32[2]{0:T(128)} %places.1, bf16[2,1,256,1152]{3,2,1,0:T(8,128)(2,1)} %refs_0_.1, ...), custom_call_target="tpu_custom_call" | custom-call | tf_op jit(solution)/shard_map/pallas_call | solution.py:445
  132.9 3.9 %shard_map.111 = (bf16[2,1,256,1152]{3,2,1,0:T(8,128)(2,1)}, bf16[2,1,256,1152]{3,2,1,0:T(8,128)(2,1)}, bf16[2,1,256,1152]{3,2,1,0:T(8,128)(2,1)}, bf16[2,1,256,1152]{3,2,1,0:T(8,128)(2,1)}, f32[72,1152]{1,0:T(8,128)}) custom-call(bf16[2,1,256,1152]{3,2,1,0:T(8,128)(2,1)} %get-tuple-element.10.refs_0_, bf16[2,1,256,1152]{3,2,1,0:T(8,128)(2,1)} %get-tuple-element.11.refs_1_, ...), custom_call_target="tpu_custom_call" | custom-call | tf_op jit(solution)/shard_map/pallas_call | solution.py:489

commit v5 on v4

--- a/solution.py
+++ b/solution.py
@@ -70,6 +70,23 @@
             device_id=(self.s + 1 - 2 * self.core, self.r),
             device_id_type=MESH,
         )
+
+    def send_half(self, first, past):
+        for core in range(2):
+
+            @pl.when(self.core == 1 - core)
+            def _():
+                for slab in range(first, past):
+                    place = slab_place(slab)
+                    if place[0] == core:
+                        pltpu.make_async_remote_copy(
+                            src_ref=self.term.at[place],
+                            dst_ref=self.half.at[place[1:]],
+                            send_sem=self.half_sems.at[0],
+                            recv_sem=self.half_sems.at[1],
+                            device_id=(self.s + 1 - 2 * self.core, self.r),
+                            device_id_type=MESH,
+                        ).start()
 
     def add_half(self):
         self.half_copy().wait()
@@ -307,11 +324,12 @@
 
         lax.fori_loop(first, past, head, 0)
 
-    def weight_term(self, term):
+    def weight_term(self, term, after):
         for cols in columns_of(self.width):
             found = dot(self.grad[:, cols], self.attn[...], (0, 0))
             for k in range(cols.size // 8):
                 term[slab_place(cols.start // 8 + k)] = found[8 * k : 8 * k + 8]
+            after(cols.start // 8, (cols.start + cols.size) // 8)
 
 
 class Exchange:
@@ -404,8 +422,7 @@
             work.project(c)
             offer(c, range(4))
     give(8)
-    work.weight_term(term)
-    weight_sum.half_copy().start()
+    work.weight_term(term, weight_sum.send_half)
     give(6)
     work.project(end)
     offer(end, [0])

time: 138 us -> 139 us (level)
  no operation moved by 1% of the time
where the time goes in v5:
time: 139 us; the launch traced here: 137 us
  Pallas kernels  136 us (98%)
    pallas_call x1, Pallas kernels, fused(): pl.pallas_call(functools.partial(fused_kernel, n, part), out_shape=[jax.S...  132 us
    pallas_call x1, Pallas kernels, deliver(): pl.pallas_call(deliver_kernel, out_shape=[jax.ShapeDtypeStruct(a.shape, a...  3.87 us

profile of v5, /device:TPU:24, one launch (start us, length us, event | category | flops | bytes accessed | tf_op | source)
XLA Modules:
  0.0 136.7 jit_solution(3730836320871343286)
XLA Ops:
  0.6 132.0 %shard_map.110 = (bf16[2,1,256,1152]{3,2,1,0:T(8,128)(2,1)}, bf16[2,1,256,1152]{3,2,1,0:T(8,128)(2,1)}, bf16[2,1,256,1152]{3,2,1,0:T(8,128)(2,1)}, bf16[2,1,256,1152]{3,2,1,0:T(8,128)(2,1)}, f32[72,1152]{1,0:T(8,128)}) custom-call(s32[2]{0:T(128)} %frames.1, s32[2]{0:T(128)} %places.1, bf16[2,1,256,1152]{3,2,1,0:T(8,128)(2,1)} %refs_0_.1, ...), custom_call_target="tpu_custom_call" | custom-call | tf_op jit(solution)/shard_map/pallas_call | solution.py:462
  132.7 3.9 %shard_map.111 = (bf16[2,1,256,1152]{3,2,1,0:T(8,128)(2,1)}, bf16[2,1,256,1152]{3,2,1,0:T(8,128)(2,1)}, bf16[2,1,256,1152]{3,2,1,0:T(8,128)(2,1)}, bf16[2,1,256,1152]{3,2,1,0:T(8,128)(2,1)}, f32[72,1152]{1,0:T(8,128)}) custom-call(bf16[2,1,256,1152]{3,2,1,0:T(8,128)(2,1)} %get-tuple-element.10.refs_0_, bf16[2,1,256,1152]{3,2,1,0:T(8,128)(2,1)} %get-tuple-element.11.refs_1_, ...), custom_call_target="tpu_custom_call" | custom-call | tf_op jit(solution)/shard_map/pallas_call | solution.py:506
